TPU v7x, 32 devices: a whole 2x2x4 slice. The times are simulated.
32 devices in a mesh: groups: 2 (over y), rows: 8 (over z, x), layers: 2 (over core).
Axes of the slice: x: 2, y: 2, z: 4, core: 2. Of those that a mesh axis runs over, the one named last changes fastest.
Arguments:
- train_grads: bfloat16 [6144, 2, 4096], P(('groups', 'rows'), 'layers'), parts along dimension 0, may hold values from -6 to 6
- query_grads: bfloat16 [2, 2048, 4096], P('layers', ('groups', 'rows')), parts along dimension 1, may hold values from -0.09375 to 0.09375
Outputs:
- scores: float32 [1024, 6144], P('layers', ('groups', 'rows')), parts along dimension 1
There are 2 independent parts, one for each index of `groups`. A program takes and returns all parts, laid end to end along the dimension named above; each array names one. Nothing has to cross between parts.
All inputs are finite; a program needn't handle non-finite values.
Results may differ from a plain program's by a relative error of at most 0.0003.
Values may be sent and summed in bfloat16 or wider, within the bound.
No kernel may reach another device: no remote copies, remote signals or barrier semaphores. Data moves between devices by JAX's collectives and lax.ppermute only.
A program may use at most 64 MiB of HBM per device.

v0:
```python
import jax
import jax.numpy as jnp
from jax import lax
from jax.sharding import PartitionSpec as P


def partial_scores(queries, train_grads):
    return jnp.einsum("lqk,nlk->qn", queries, train_grads, preferred_element_type=jnp.float32)


def shards(train_grads, query_grads):
    terms = partial_scores(lax.all_gather(query_grads, "rows", axis=1, tiled=True), train_grads)
    return lax.psum_scatter(terms, "layers", scatter_dimension=0, tiled=True)


def solution(mesh):
    in_specs = (P(("groups", "rows"), "layers", None), P("layers", ("groups", "rows"), None))
    out_specs = P("layers", ("groups", "rows"))
    return jax.shard_map(shards, mesh=mesh, in_specs=in_specs, out_specs=out_specs, check_vma=False)
```

profile of v0, /device:TPU:0, one launch (start us, length us, event | category | flops | bytes accessed | tf_op | source)
XLA Modules:
  0.0 159.1 jit_solution(11661200120718518420)
XLA Ops:
  6.5 0.0 copy-start
  6.5 0.0 all-gather.2.cloned.1.call-start
  6.5 0.7 all-gather.2.cloned.1.call-update
  7.3 0.0 reduce-scatter.2.cloned.1.call-start
  7.3 129.4 %all-gather.2.cloned.1.call-done = bf16[1,1024,4096]{2,1,0:T(8,128)(2,1)} async-done(((bf16[1,128,4096]{2,1,0:T(8,128)(2,1)}), bf16[1,1024,4096]{2,1,0:T(8,128)(2,1)}) %all-gather.2.cloned.1.call-update) | async-done | bytes 8388624 | tf_op jit(solution)/shard_map/all_gather | solution.py:12
  136.7 0.0 copy-done
  136.7 8.1 %fusion = f32[1024,384]{1,0:T(8,128)} fusion(bf16[1,1024,4096]{2,1,0:T(8,128)(2,1)} %all-gather.2.cloned.1.call-done, bf16[384,1,4096]{2,0,1:T(8,128)(2,1)S(1)} %copy-done), kind=kOutput, calls=%fused_computation | convolution fusion | flops 3221225472 | bytes 13107200 | tf_op jit(solution)/shard_map/lqk,nlk->qn/dot_general | solution.py:8
  144.8 0.0 reduce-scatter.2.cloned.1.call-update
  144.8 7.4 %reduce-scatter.2.cloned.1.call-done = f32[512,384]{1,0:T(8,128)} async-done(((f32[1024,384]{1,0:T(8,128)}), f32[512,384]{1,0:T(8,128)}) %reduce-scatter.2.cloned.1.call-update) | async-done | bytes 786448 | tf_op jit(solution)/shard_map/reduce_scatter | solution.py:13
Async XLA Ops:
  6.5 130.2 %copy-start = (bf16[384,1,4096]{2,0,1:T(8,128)(2,1)S(1)}, bf16[384,1,4096]{2,0,1:T(8,128)(2,1)}, u32[]{:S(2)}) copy-start(bf16[384,1,4096]{2,0,1:T(8,128)(2,1)} %param.2) | copy-start | bytes 9437188
  6.5 130.1 %all-gather.2.cloned.1.call-start = ((), (), s32[]{:S(2)}) async-start(), calls=%async_computation.1 | async-start | bytes 9437184 | tf_op jit(solution)/shard_map/all_gather | solution.py:12
  7.3 145.0 %reduce-scatter.2.cloned.1.call-start = ((), (), s32[]{:S(2)}) async-start(), calls=%async_computation.2 | async-start | bytes 2359296 | tf_op jit(solution)/shard_map/reduce_scatter | solution.py:13
Sparse Core Ops, SparseCore 0:
  9.5 127.1 all-gather.1
  145.0 7.2 reduce-scatter.1
where the time goes:
time: 159 us
  waiting for transfers between devices  137 us (86%)
  between operations  13.4 us (8%)
  matrix products  8.13 us (5%)
    all_gather x1, waiting for transfers between devices, shards(): lax.all_gather(query_grads, 'rows', axis=1, tiled=True)  129 us
    dot_general x1, matrix products, partial_scores(): jnp.einsum('lqk,nlk->qn', queries, train_grads, preferred_element_type=jn...  8.13 us
    reduce_scatter x1, waiting for transfers between devices, shards(): return lax.psum_scatter(terms, 'layers', scatter_dimension=0, tiled=True)  7.37 us
  transfers between devices with their start and end apart: 2, of which 2 were waited for; matrix products, arithmetic and copies ran while one was open for 0% of the time, Pallas kernels for 0%

commit v1 on v0

v1 whole, which is shorter than its diff:
```python
import functools

import jax
import jax.numpy as jnp
import numpy as np
from jax import lax
from jax.experimental import pallas as pl
from jax.experimental.pallas import tpu as pltpu
from jax.sharding import PartitionSpec as P


NT = (((1,), (1,)), ((), ()))


def product(left, right):
    return lax.dot_general(left, right, NT, preferred_element_type=jnp.float32)


def place_rows(count, blocks, me_ref, table_ref, *refs):
    out_ref = refs[-1]
    rows = refs[0].shape[0]
    first = me_ref[1] * blocks
    for slot in range(count):
        block = table_ref[me_ref[0], slot] - first

        @pl.when((block >= 0) & (block < blocks))
        def _(slot=slot, block=block):
            at = pl.multiple_of(block * rows, rows)
            out_ref[pl.ds(at, rows), :] = refs[2 * slot][...] + refs[2 * slot + 1][...]


def shards(train_grads, query_grads):
    rows, layers = lax.axis_size("rows"), lax.axis_size("layers")
    train = train_grads.reshape(train_grads.shape[0], -1)
    queries = jnp.swapaxes(query_grads, 0, 1).reshape(query_grads.shape[1], -1)
    size, depth = queries.shape
    count = rows // 2

    ring = [2 * z for z in range(count)] + [2 * z + 1 for z in reversed(range(count))]
    ahead = [(ring[i], ring[(i + 1) % rows]) for i in range(rows)]
    back = [(target, source) for source, target in ahead]
    place = {row: i for i, row in enumerate(ring)}

    half = depth // 2
    right, left = [queries[:, :half], queries[:, half:]], [queries[:, :half], queries[:, half:]]

    def scores(pieces):
        return product(pieces[0], train[:, :half]) + product(pieces[1], train[:, half:])

    def move(piece, pairs):
        return lax.ppermute(piece, "rows", pairs)

    sums, offsets = [product(queries, train)], [0]
    for step in range(1, count + 1):
        if step < count:
            right = [move(piece, ahead) for piece in right]
            left = [move(piece, back) for piece in left]
            sums += [scores(right), scores(left)]
            offsets += [-step, step]
        else:
            last = [move(right[0], ahead), move(left[1], back)]
            sums.append(scores(last))
            offsets.append(step)

    table = np.array([[ring[(place[row] + by) % rows] for by in offsets] for row in range(rows)], np.int32)
    me = jnp.stack([lax.axis_index("rows"), lax.axis_index("layers")]).astype(jnp.int32)
    if layers != 2:
        total = jnp.zeros((rows * size, train.shape[0]), jnp.float32)
        for slot, value in enumerate(sums):
            total = lax.dynamic_update_slice_in_dim(total, value, jnp.asarray(table)[me[0], slot] * size, 0)
        return lax.psum_scatter(total, "layers", scatter_dimension=0, tiled=True)
    operands = []
    for value in sums:
        operands += [value, lax.ppermute(value, "layers", [(0, 1), (1, 0)])]
    return pl.pallas_call(
        functools.partial(place_rows, len(sums), rows // layers),
        out_shape=jax.ShapeDtypeStruct((rows * size // layers, train.shape[0]), jnp.float32),
        in_specs=[pl.BlockSpec(memory_space=pltpu.SMEM)] * 2 + [pl.BlockSpec(memory_space=pltpu.VMEM)] * len(operands),
        out_specs=pl.BlockSpec(memory_space=pltpu.VMEM),
    )(me, table, *operands)


def solution(mesh):
    in_specs = (P(("groups", "rows"), "layers", None), P("layers", ("groups", "rows"), None))
    out_specs = P("layers", ("groups", "rows"))
    return jax.shard_map(shards, mesh=mesh, in_specs=in_specs, out_specs=out_specs, check_vma=False)
```

time: 159 us -> 111 us (0.70)
  waiting for transfers between devices: 137 us -> 71 us
  starting transfers between devices: 0.04 us -> 21.3 us
  between operations: 13.4 us -> 0.37 us
  matrix products: 8.13 us -> 11.6 us
  Pallas kernels: 0 us -> 3 us
  local copies, waits for them, and re-layouts: 0.01 us -> 2.5 us
    all_gather x1 -> x0, waiting for transfers between devices: 129 us -> none  [shards(): lax.all_gather(query_grads, 'rows', axis=1, tiled=True)]
    ppermute x0 -> x22, waiting for transfers between devices: none -> 71 us  [the longest x14 70.2 us: move(): return lax.ppermute(piece, 'rows', pairs)]
    ppermute x0 -> x22, starting transfers between devices: none -> 21.3 us  [the longest x14 19.9 us: move(): return lax.ppermute(piece, 'rows', pairs)]
    reduce_scatter x1 -> x0, waiting for transfers between devices: 7.37 us -> none  [shards(): return lax.psum_scatter(terms, 'layers', scatter_dimension=0, tiled=True)]
    dot_general x1 -> x15, matrix products: 8.13 us -> 11.6 us  [product(): return lax.dot_general(left, right, NT, preferred_element_type=jnp.float32)]
    pallas_call x0 -> x1, Pallas kernels: none -> 3 us  [shards(): pl.pallas_call(functools.partial(place_rows, len(sums), rows // layers),...]
  transfers between devices with their start and end apart: 2 -> 22, of which waited for: 2 -> 11; matrix products, arithmetic and copies ran while one was open for 0% -> 11% of each run, Pallas kernels for 0% -> 0%
where the time goes in v1:
time: 111 us; the launch traced here: 110 us
  waiting for transfers between devices  71 us (64%)
  starting transfers between devices  21.3 us (19%)
  matrix products  11.6 us (10%)
  Pallas kernels  3 us (3%)
  local copies, waits for them, and re-layouts  2.5 us (2%)
    ppermute x14, waiting for transfers between devices, move(): return lax.ppermute(piece, 'rows', pairs)  70.2 us
    ppermute x14, starting transfers between devices, move(): return lax.ppermute(piece, 'rows', pairs)  19.9 us
    dot_general x15, matrix products, product(): return lax.dot_general(left, right, NT, preferred_element_type=jnp.float32)  11.6 us
    pallas_call x1, Pallas kernels, shards(): pl.pallas_call(functools.partial(place_rows, len(sums), rows // layers),...  3 us
  transfers between devices with their start and end apart: 22, of which 11 were waited for; matrix products, arithmetic and copies ran while one was open for 11% of the time, Pallas kernels for 0%

profile of v1, /device:TPU:0, one launch (start us, length us, event | category | flops | bytes accessed | tf_op | source)
XLA Modules:
  0.0 110.4 jit_solution(7266774814263325469)
XLA Ops:
  0.0 1.4 %fusion.24 = (bf16[128,2048]{1,0:T(8,128)(2,1)S(1)}, bf16[128,2048]{1,0:T(8,128)(2,1)S(1)}) fusion(bf16[128,4096]{1,0:T(8,128)(2,1)} %bitcast.22), kind=kLoop, calls=%fused_computation.32 | loop fusion | bytes 2097152 | tf_op jit(solution)/shard_map/slice | solution.py:45
  1.4 3.1 %collective-permute-start.2 = (bf16[128,2048]{1,0:T(8,128)(2,1)S(1)}, bf16[128,2048]{1,0:T(8,128)(2,1)S(1)}, u32[]{:S(2)}, u32[]{:S(2)}) collective-permute-start(bf16[128,2048]{1,0:T(8,128)(2,1)S(1)} %get-tuple-element.6), channel_id=1, source_target_pairs={{0,4},{4,8},{8,12},{12,14},{14,10},{10,6},{6,2},{2,0},{1,5},{5,9},... | collective-permute-start | bytes 1572872 | tf_op jit(solution)/shard_map/ppermute | solution.py:51
  4.5 2.0 %collective-permute-start.1 = (bf16[128,2048]{1,0:T(8,128)(2,1)S(1)}, bf16[128,2048]{1,0:T(8,128)(2,1)S(1)}, u32[]{:S(2)}, u32[]{:S(2)}) collective-permute-start(bf16[128,2048]{1,0:T(8,128)(2,1)S(1)} %get-tuple-element.5), channel_id=1, source_target_pairs={{0,4},{4,8},{8,12},{12,14},{14,10},{10,6},{6,2},{2,0},{1,5},{5,9},... | collective-permute-start | bytes 1572872 | tf_op jit(solution)/shard_map/ppermute | solution.py:51
  6.6 3.3 %fusion.21.refs_0_ = f32[128,384]{1,0:T(8,128)S(1)} fusion(bf16[384,1,4096]{2,0,1:T(8,128)(2,1)} %param.3, bf16[1,128,4096]{2,1,0:T(8,128)(2,1)} %param.4), kind=kOutput, calls=%fused_computation.29 | convolution fusion | flops 402653184 | bytes 4390912 | tf_op jit(solution)/shard_map/dot_general | solution.py:16
  9.9 7.3 %collective-permute-done.2 = bf16[128,2048]{1,0:T(8,128)(2,1)S(1)} collective-permute-done((bf16[128,2048]{1,0:T(8,128)(2,1)S(1)}, bf16[128,2048]{1,0:T(8,128)(2,1)S(1)}, u32[]{:S(2)}, u32[]{:S(2)}) %collective-permute-start.2) | collective-permute-done | bytes 524320 | tf_op jit(solution)/shard_map/ppermute | solution.py:51
  17.2 0.6 fusion.12
  17.8 9.8 %collective-permute-done.1 = bf16[128,2048]{1,0:T(8,128)(2,1)S(1)} collective-permute-done((bf16[128,2048]{1,0:T(8,128)(2,1)S(1)}, bf16[128,2048]{1,0:T(8,128)(2,1)S(1)}, u32[]{:S(2)}, u32[]{:S(2)}) %collective-permute-start.1) | collective-permute-done | bytes 524320 | tf_op jit(solution)/shard_map/ppermute | solution.py:51
  27.6 0.6 convolution_add_fusion.6.refs_2_
  28.2 0.1 collective-permute-start.3
  28.3 1.9 %collective-permute-start.8 = (bf16[128,2048]{1,0:T(8,128)(2,1)S(1)}, bf16[128,2048]{1,0:T(8,128)(2,1)S(1)}, u32[]{:S(2)}, u32[]{:S(2)}) collective-permute-start(bf16[128,2048]{1,0:T(8,128)(2,1)S(1)} %collective-permute-done.2), channel_id=1, source_target_pairs={{0,4},{4,8},{8,12},{12,14},{14,10},{10,6},{6,2},{2,0},{1,5},{5,9},... | collective-permute-start | bytes 1572872 | tf_op jit(solution)/shard_map/ppermute | solution.py:51
  30.2 1.6 %collective-permute-start.7 = (bf16[128,2048]{1,0:T(8,128)(2,1)S(1)}, bf16[128,2048]{1,0:T(8,128)(2,1)S(1)}, u32[]{:S(2)}, u32[]{:S(2)}) collective-permute-start(bf16[128,2048]{1,0:T(8,128)(2,1)S(1)} %collective-permute-done.1), channel_id=1, source_target_pairs={{0,4},{4,8},{8,12},{12,14},{14,10},{10,6},{6,2},{2,0},{1,5},{5,9},... | collective-permute-start | bytes 1572872 | tf_op jit(solution)/shard_map/ppermute | solution.py:51
  31.8 0.6 fusion.10
  32.4 0.5 collective-permute-start.11
  32.9 0.6 convolution_add_fusion.5.refs_4_
  33.5 9.6 %collective-permute-done.8 = bf16[128,2048]{1,0:T(8,128)(2,1)S(1)} collective-permute-done((bf16[128,2048]{1,0:T(8,128)(2,1)S(1)}, bf16[128,2048]{1,0:T(8,128)(2,1)S(1)}, u32[]{:S(2)}, u32[]{:S(2)}) %collective-permute-start.8) | collective-permute-done | bytes 524320 | tf_op jit(solution)/shard_map/ppermute | solution.py:51
  43.1 1.7 %collective-permute-start.10 = (bf16[128,2048]{1,0:T(8,128)(2,1)S(1)}, bf16[128,2048]{1,0:T(8,128)(2,1)S(1)}, u32[]{:S(2)}, u32[]{:S(2)}) collective-permute-start(bf16[128,2048]{1,0:T(8,128)(2,1)S(1)} %collective-permute-done.4), channel_id=1, source_target_pairs={{4,0},{8,4},{12,8},{14,12},{10,14},{6,10},{2,6},{0,2},{5,1},{9,5},... | collective-permute-start | bytes 1572872 | tf_op jit(solution)/shard_map/ppermute | solution.py:51
  44.9 0.6 fusion.8
  45.5 8.4 %collective-permute-done.7 = bf16[128,2048]{1,0:T(8,128)(2,1)S(1)} collective-permute-done((bf16[128,2048]{1,0:T(8,128)(2,1)S(1)}, bf16[128,2048]{1,0:T(8,128)(2,1)S(1)}, u32[]{:S(2)}, u32[]{:S(2)}) %collective-permute-start.7) | collective-permute-done | bytes 524320 | tf_op jit(solution)/shard_map/ppermute | solution.py:51
  53.9 1.8 %collective-permute-start.14 = (bf16[128,2048]{1,0:T(8,128)(2,1)S(1)}, bf16[128,2048]{1,0:T(8,128)(2,1)S(1)}, u32[]{:S(2)}, u32[]{:S(2)}) collective-permute-start(bf16[128,2048]{1,0:T(8,128)(2,1)S(1)} %collective-permute-done.8), channel_id=1, source_target_pairs={{0,4},{4,8},{8,12},{12,14},{14,10},{10,6},{6,2},{2,0},{1,5},{5,9},... | collective-permute-start | bytes 1572872 | tf_op jit(solution)/shard_map/ppermute | solution.py:51
  55.7 0.6 convolution_add_fusion.4.refs_6_
  56.3 1.6 %collective-permute-start.13 = (bf16[128,2048]{1,0:T(8,128)(2,1)S(1)}, bf16[128,2048]{1,0:T(8,128)(2,1)S(1)}, u32[]{:S(2)}, u32[]{:S(2)}) collective-permute-start(bf16[128,2048]{1,0:T(8,128)(2,1)S(1)} %collective-permute-done.7), channel_id=1, source_target_pairs={{0,4},{4,8},{8,12},{12,14},{14,10},{10,6},{6,2},{2,0},{1,5},{5,9},... | collective-permute-start | bytes 1572872 | tf_op jit(solution)/shard_map/ppermute | solution.py:51
  57.9 0.6 fusion.6
  58.6 0.5 collective-permute-start.17
  59.1 0.6 convolution_add_fusion.3.refs_8_
  59.7 9.0 %collective-permute-done.14 = bf16[128,2048]{1,0:T(8,128)(2,1)S(1)} collective-permute-done((bf16[128,2048]{1,0:T(8,128)(2,1)S(1)}, bf16[128,2048]{1,0:T(8,128)(2,1)S(1)}, u32[]{:S(2)}, u32[]{:S(2)}) %collective-permute-start.14) | collective-permute-done | bytes 524320 | tf_op jit(solution)/shard_map/ppermute | solution.py:51
  68.7 0.6 fusion.4
  69.3 9.2 %collective-permute-done.13 = bf16[128,2048]{1,0:T(8,128)(2,1)S(1)} collective-permute-done((bf16[128,2048]{1,0:T(8,128)(2,1)S(1)}, bf16[128,2048]{1,0:T(8,128)(2,1)S(1)}, u32[]{:S(2)}, u32[]{:S(2)}) %collective-permute-start.13) | collective-permute-done | bytes 524320 | tf_op jit(solution)/shard_map/ppermute | solution.py:51
  78.5 1.7 %collective-permute-start.16 = (bf16[128,2048]{1,0:T(8,128)(2,1)S(1)}, bf16[128,2048]{1,0:T(8,128)(2,1)S(1)}, u32[]{:S(2)}, u32[]{:S(2)}) collective-permute-start(bf16[128,2048]{1,0:T(8,128)(2,1)S(1)} %collective-permute-done.10), channel_id=1, source_target_pairs={{4,0},{8,4},{12,8},{14,12},{10,14},{6,10},{2,6},{0,2},{5,1},{9,5},... | collective-permute-start | bytes 1572872 | tf_op jit(solution)/shard_map/ppermute | solution.py:51
  80.3 1.6 %collective-permute-start.20 = (bf16[128,2048]{1,0:T(8,128)(2,1)S(1)}, bf16[128,2048]{1,0:T(8,128)(2,1)S(1)}, u32[]{:S(2)}, u32[]{:S(2)}) collective-permute-start(bf16[128,2048]{1,0:T(8,128)(2,1)S(1)} %collective-permute-done.17), channel_id=1, source_target_pairs={{4,0},{8,4},{12,8},{14,12},{10,14},{6,10},{2,6},{0,2},{5,1},{9,5},... | collective-permute-start | bytes 1572872 | tf_op jit(solution)/shard_map/ppermute | solution.py:51
  81.8 0.6 convolution_add_fusion.2.refs_10_
  82.5 0.6 fusion.2
  83.1 10.3 %collective-permute-done.16 = bf16[128,2048]{1,0:T(8,128)(2,1)S(1)} collective-permute-done((bf16[128,2048]{1,0:T(8,128)(2,1)S(1)}, bf16[128,2048]{1,0:T(8,128)(2,1)S(1)}, u32[]{:S(2)}, u32[]{:S(2)}) %collective-permute-start.16) | collective-permute-done | bytes 524320 | tf_op jit(solution)/shard_map/ppermute | solution.py:51
  93.3 1.8 %collective-permute-start.19 = (bf16[128,2048]{1,0:T(8,128)(2,1)S(1)}, bf16[128,2048]{1,0:T(8,128)(2,1)S(1)}, u32[]{:S(2)}, u32[]{:S(2)}) collective-permute-start(bf16[128,2048]{1,0:T(8,128)(2,1)S(1)} %collective-permute-done.13), channel_id=1, source_target_pairs={{0,4},{4,8},{8,12},{12,14},{14,10},{10,6},{6,2},{2,0},{1,5},{5,9},... | collective-permute-start | bytes 1572872 | tf_op jit(solution)/shard_map/ppermute | solution.py:51
  95.1 0.6 convolution_add_fusion.1.refs_12_
  95.7 6.6 %collective-permute-done.20 = bf16[128,2048]{1,0:T(8,128)(2,1)S(1)} collective-permute-done((bf16[128,2048]{1,0:T(8,128)(2,1)S(1)}, bf16[128,2048]{1,0:T(8,128)(2,1)S(1)}, u32[]{:S(2)}, u32[]{:S(2)}) %collective-permute-start.20) | collective-permute-done | bytes 524320 | tf_op jit(solution)/shard_map/ppermute | solution.py:51
  102.4 0.6 fusion
  103.0 0.6 collective-permute-start.12
  103.6 0.6 convolution_add_fusion.refs_14_
  104.2 0.1 collective-permute-start.15
  104.3 0.5 collective-permute-start.18
  104.8 0.1 collective-permute-start.21
  104.9 0.6 pad_add_fusion.me_ref
  105.6 0.2 collective-permute-done.15.refs_11_
  105.7 0.3 collective-permute-done.18.refs_13_
  106.0 0.3 collective-permute-done.21.refs_15_
  106.4 0.3 copy-done.15
  106.7 0.7 copy-done.16
  107.4 3.0 %shard_map.37 = f32[512,384]{1,0:T(8,128)} custom-call(s32[2]{0:T(128)} %pad_add_fusion.me_ref, s32[8,8]{1,0:T(8,128)} %constant.10.clone.table_ref, f32[128,384]{1,0:T(8,128)} %copy-done.1, f32[128,384]{1,0:T(8,128)} %copy-done.2, f32[128,384]{1,0:T(8,128)} %copy-done.3, f32[128,384]{1,0:T(8,128)} %copy-done.4, f32[128,384]{1,0:T(8,128)} %copy-done.5, ...), custom_call_target="tpu_custom_call" | custom-call | tf_op jit(solution)/shard_map/pallas_call | solution.py:75
  (48 shorter events, 0.2 us)
Async XLA Ops:
  0.0 17.2 %copy-start = (bf16[384,1,4096]{2,0,1:T(8,128)(2,1)S(1)}, bf16[384,1,4096]{2,0,1:T(8,128)(2,1)}, u32[]{:S(2)}) copy-start(bf16[384,1,4096]{2,0,1:T(8,128)(2,1)} %param.3) | copy-start | bytes 9437188
  1.4 15.8 %collective-permute-start.2 = (bf16[128,2048]{1,0:T(8,128)(2,1)S(1)}, bf16[128,2048]{1,0:T(8,128)(2,1)S(1)}, u32[]{:S(2)}, u32[]{:S(2)}) collective-permute-start(bf16[128,2048]{1,0:T(8,128)(2,1)S(1)} %get-tuple-element.6), channel_id=1, source_target_pairs={{0,4},{4,8},{8,12},{12,14},{14,10},{10,6},{6,2},{2,0},{1,5},{5,9},... | collective-permute-start | bytes 1572872 | tf_op jit(solution)/shard_map/ppermute | solution.py:51
  4.5 25.7 %collective-permute-start.5 = (bf16[128,2048]{1,0:T(8,128)(2,1)S(1)}, bf16[128,2048]{1,0:T(8,128)(2,1)S(1)}, u32[]{:S(2)}, u32[]{:S(2)}) collective-permute-start(bf16[128,2048]{1,0:T(8,128)(2,1)S(1)} %get-tuple-element.6), channel_id=1, source_target_pairs={{4,0},{8,4},{12,8},{14,12},{10,14},{6,10},{2,6},{0,2},{5,1},{9,5},... | collective-permute-start | bytes 1572872 | tf_op jit(solution)/shard_map/ppermute | solution.py:51
  4.5 23.1 %collective-permute-start.1 = (bf16[128,2048]{1,0:T(8,128)(2,1)S(1)}, bf16[128,2048]{1,0:T(8,128)(2,1)S(1)}, u32[]{:S(2)}, u32[]{:S(2)}) collective-permute-start(bf16[128,2048]{1,0:T(8,128)(2,1)S(1)} %get-tuple-element.5), channel_id=1, source_target_pairs={{0,4},{4,8},{8,12},{12,14},{14,10},{10,6},{6,2},{2,0},{1,5},{5,9},... | collective-permute-start | bytes 1572872 | tf_op jit(solution)/shard_map/ppermute | solution.py:51
  6.6 25.8 %collective-permute-start.4 = (bf16[128,2048]{1,0:T(8,128)(2,1)S(1)}, bf16[128,2048]{1,0:T(8,128)(2,1)S(1)}, u32[]{:S(2)}, u32[]{:S(2)}) collective-permute-start(bf16[128,2048]{1,0:T(8,128)(2,1)S(1)} %get-tuple-element.5), channel_id=1, source_target_pairs={{4,0},{8,4},{12,8},{14,12},{10,14},{6,10},{2,6},{0,2},{5,1},{9,5},... | collective-permute-start | bytes 1572872 | tf_op jit(solution)/shard_map/ppermute | solution.py:51
  9.8 22.5 %copy-start.1 = (f32[128,384]{1,0:T(8,128)}, f32[128,384]{1,0:T(8,128)S(1)}, u32[]{:S(2)}) copy-start(f32[128,384]{1,0:T(8,128)S(1)} %fusion.21.refs_0_) | copy-start | bytes 589828
  9.8 94.4 %collective-permute-start = (f32[128,384]{1,0:T(8,128)S(1)}, f32[128,384]{1,0:T(8,128)S(1)}, u32[]{:S(2)}, u32[]{:S(2)}) collective-permute-start(f32[128,384]{1,0:T(8,128)S(1)} %fusion.21.refs_0_), channel_id=1, source_target_pairs={{0,1},{1,0},{2,3},{3,2},{4,5},{5,4},{6,7},{7,6},{8,9},{9,8},{10,11... | collective-permute-start | bytes 589832 | tf_op jit(solution)/shard_map/ppermute | solution.py:74
  28.2 17.3 %copy-start.3 = (f32[128,384]{1,0:T(8,128)}, f32[128,384]{1,0:T(8,128)S(1)}, u32[]{:S(2)}) copy-start(f32[128,384]{1,0:T(8,128)S(1)} %convolution_add_fusion.6.refs_2_) | copy-start | bytes 589828
  28.2 76.1 %collective-permute-start.3 = (f32[128,384]{1,0:T(8,128)S(1)}, f32[128,384]{1,0:T(8,128)S(1)}, u32[]{:S(2)}, u32[]{:S(2)}) collective-permute-start(f32[128,384]{1,0:T(8,128)S(1)} %convolution_add_fusion.6.refs_2_), channel_id=1, source_target_pairs={{0,1},{1,0},{2,3},{3,2},{4,5},{5,4},{6,7},{7,6},{8,9},{9,8},{10,11... | collective-permute-start | bytes 589832 | tf_op jit(solution)/shard_map/ppermute | solution.py:74
  28.3 14.8 %collective-permute-start.8 = (bf16[128,2048]{1,0:T(8,128)(2,1)S(1)}, bf16[128,2048]{1,0:T(8,128)(2,1)S(1)}, u32[]{:S(2)}, u32[]{:S(2)}) collective-permute-start(bf16[128,2048]{1,0:T(8,128)(2,1)S(1)} %collective-permute-done.2), channel_id=1, source_target_pairs={{0,4},{4,8},{8,12},{12,14},{14,10},{10,6},{6,2},{2,0},{1,5},{5,9},... | collective-permute-start | bytes 1572872 | tf_op jit(solution)/shard_map/ppermute | solution.py:51
  30.2 23.7 %collective-permute-start.7 = (bf16[128,2048]{1,0:T(8,128)(2,1)S(1)}, bf16[128,2048]{1,0:T(8,128)(2,1)S(1)}, u32[]{:S(2)}, u32[]{:S(2)}) collective-permute-start(bf16[128,2048]{1,0:T(8,128)(2,1)S(1)} %collective-permute-done.1), channel_id=1, source_target_pairs={{0,4},{4,8},{8,12},{12,14},{14,10},{10,6},{6,2},{2,0},{1,5},{5,9},... | collective-permute-start | bytes 1572872 | tf_op jit(solution)/shard_map/ppermute | solution.py:51
  32.4 23.9 %collective-permute-start.11 = (bf16[128,2048]{1,0:T(8,128)(2,1)S(1)}, bf16[128,2048]{1,0:T(8,128)(2,1)S(1)}, u32[]{:S(2)}, u32[]{:S(2)}) collective-permute-start(bf16[128,2048]{1,0:T(8,128)(2,1)S(1)} %collective-permute-done.5), channel_id=1, source_target_pairs={{4,0},{8,4},{12,8},{14,12},{10,14},{6,10},{2,6},{0,2},{5,1},{9,5},... | collective-permute-start | bytes 1572872 | tf_op jit(solution)/shard_map/ppermute | solution.py:51
  33.5 35.2 %copy-start.5 = (f32[128,384]{1,0:T(8,128)}, f32[128,384]{1,0:T(8,128)S(1)}, u32[]{:S(2)}) copy-start(f32[128,384]{1,0:T(8,128)S(1)} %convolution_add_fusion.5.refs_4_) | copy-start | bytes 589828
  43.1 15.4 %collective-permute-start.10 = (bf16[128,2048]{1,0:T(8,128)(2,1)S(1)}, bf16[128,2048]{1,0:T(8,128)(2,1)S(1)}, u32[]{:S(2)}, u32[]{:S(2)}) collective-permute-start(bf16[128,2048]{1,0:T(8,128)(2,1)S(1)} %collective-permute-done.4), channel_id=1, source_target_pairs={{4,0},{8,4},{12,8},{14,12},{10,14},{6,10},{2,6},{0,2},{5,1},{9,5},... | collective-permute-start | bytes 1572872 | tf_op jit(solution)/shard_map/ppermute | solution.py:51
  53.9 14.8 %collective-permute-start.14 = (bf16[128,2048]{1,0:T(8,128)(2,1)S(1)}, bf16[128,2048]{1,0:T(8,128)(2,1)S(1)}, u32[]{:S(2)}, u32[]{:S(2)}) collective-permute-start(bf16[128,2048]{1,0:T(8,128)(2,1)S(1)} %collective-permute-done.8), channel_id=1, source_target_pairs={{0,4},{4,8},{8,12},{12,14},{14,10},{10,6},{6,2},{2,0},{1,5},{5,9},... | collective-permute-start | bytes 1572872 | tf_op jit(solution)/shard_map/ppermute | solution.py:51
  56.3 46.1 %copy-start.6 = (f32[128,384]{1,0:T(8,128)}, f32[128,384]{1,0:T(8,128)S(1)}, u32[]{:S(2)}) copy-start(f32[128,384]{1,0:T(8,128)S(1)} %convolution_add_fusion.4.refs_6_) | copy-start | bytes 589828
  56.3 22.2 %collective-permute-start.13 = (bf16[128,2048]{1,0:T(8,128)(2,1)S(1)}, bf16[128,2048]{1,0:T(8,128)(2,1)S(1)}, u32[]{:S(2)}, u32[]{:S(2)}) collective-permute-start(bf16[128,2048]{1,0:T(8,128)(2,1)S(1)} %collective-permute-done.7), channel_id=1, source_target_pairs={{0,4},{4,8},{8,12},{12,14},{14,10},{10,6},{6,2},{2,0},{1,5},{5,9},... | collective-permute-start | bytes 1572872 | tf_op jit(solution)/shard_map/ppermute | solution.py:51
  58.6 21.7 %collective-permute-start.17 = (bf16[128,2048]{1,0:T(8,128)(2,1)S(1)}, bf16[128,2048]{1,0:T(8,128)(2,1)S(1)}, u32[]{:S(2)}, u32[]{:S(2)}) collective-permute-start(bf16[128,2048]{1,0:T(8,128)(2,1)S(1)} %collective-permute-done.11), channel_id=1, source_target_pairs={{4,0},{8,4},{12,8},{14,12},{10,14},{6,10},{2,6},{0,2},{5,1},{9,5},... | collective-permute-start | bytes 1572872 | tf_op jit(solution)/shard_map/ppermute | solution.py:51
  59.7 43.4 %copy-start.7 = (f32[128,384]{1,0:T(8,128)}, f32[128,384]{1,0:T(8,128)S(1)}, u32[]{:S(2)}) copy-start(f32[128,384]{1,0:T(8,128)S(1)} %convolution_add_fusion.3.refs_8_) | copy-start | bytes 589828
  68.7 36.2 %collective-permute-start.6 = (f32[128,384]{1,0:T(8,128)S(1)}, f32[128,384]{1,0:T(8,128)S(1)}, u32[]{:S(2)}, u32[]{:S(2)}) collective-permute-start(f32[128,384]{1,0:T(8,128)S(1)} %convolution_add_fusion.5.refs_4_), channel_id=1, source_target_pairs={{0,1},{1,0},{2,3},{3,2},{4,5},{5,4},{6,7},{7,6},{8,9},{9,8},{10,11... | collective-permute-start | bytes 589832 | tf_op jit(solution)/shard_map/ppermute | solution.py:74
  78.5 14.8 %collective-permute-start.16 = (bf16[128,2048]{1,0:T(8,128)(2,1)S(1)}, bf16[128,2048]{1,0:T(8,128)(2,1)S(1)}, u32[]{:S(2)}, u32[]{:S(2)}) collective-permute-start(bf16[128,2048]{1,0:T(8,128)(2,1)S(1)} %collective-permute-done.10), channel_id=1, source_target_pairs={{4,0},{8,4},{12,8},{14,12},{10,14},{6,10},{2,6},{0,2},{5,1},{9,5},... | collective-permute-start | bytes 1572872 | tf_op jit(solution)/shard_map/ppermute | solution.py:51
  80.3 22.1 %collective-permute-start.20 = (bf16[128,2048]{1,0:T(8,128)(2,1)S(1)}, bf16[128,2048]{1,0:T(8,128)(2,1)S(1)}, u32[]{:S(2)}, u32[]{:S(2)}) collective-permute-start(bf16[128,2048]{1,0:T(8,128)(2,1)S(1)} %collective-permute-done.17), channel_id=1, source_target_pairs={{4,0},{8,4},{12,8},{14,12},{10,14},{6,10},{2,6},{0,2},{5,1},{9,5},... | collective-permute-start | bytes 1572872 | tf_op jit(solution)/shard_map/ppermute | solution.py:51
  82.4 21.8 %copy-start.9 = (f32[128,384]{1,0:T(8,128)}, f32[128,384]{1,0:T(8,128)S(1)}, u32[]{:S(2)}) copy-start(f32[128,384]{1,0:T(8,128)S(1)} %convolution_add_fusion.2.refs_10_) | copy-start | bytes 589828
  93.3 9.7 %collective-permute-start.19 = (bf16[128,2048]{1,0:T(8,128)(2,1)S(1)}, bf16[128,2048]{1,0:T(8,128)(2,1)S(1)}, u32[]{:S(2)}, u32[]{:S(2)}) collective-permute-start(bf16[128,2048]{1,0:T(8,128)(2,1)S(1)} %collective-permute-done.13), channel_id=1, source_target_pairs={{0,4},{4,8},{8,12},{12,14},{14,10},{10,6},{6,2},{2,0},{1,5},{5,9},... | collective-permute-start | bytes 1572872 | tf_op jit(solution)/shard_map/ppermute | solution.py:51
  95.7 10.6 %copy-start.10 = (f32[128,384]{1,0:T(8,128)}, f32[128,384]{1,0:T(8,128)S(1)}, u32[]{:S(2)}) copy-start(f32[128,384]{1,0:T(8,128)S(1)} %convolution_add_fusion.1.refs_12_) | copy-start | bytes 589828
  102.4 3.2 %collective-permute-start.9 = (f32[128,384]{1,0:T(8,128)S(1)}, f32[128,384]{1,0:T(8,128)S(1)}, u32[]{:S(2)}, u32[]{:S(2)}) collective-permute-start(f32[128,384]{1,0:T(8,128)S(1)} %convolution_add_fusion.4.refs_6_), channel_id=1, source_target_pairs={{0,1},{1,0},{2,3},{3,2},{4,5},{5,4},{6,7},{7,6},{8,9},{9,8},{10,11... | collective-permute-start | bytes 589832 | tf_op jit(solution)/shard_map/ppermute | solution.py:74
  103.0 2.5 %collective-permute-start.12 = (f32[128,384]{1,0:T(8,128)S(1)}, f32[128,384]{1,0:T(8,128)S(1)}, u32[]{:S(2)}, u32[]{:S(2)}) collective-permute-start(f32[128,384]{1,0:T(8,128)S(1)} %convolution_add_fusion.3.refs_8_), channel_id=1, source_target_pairs={{0,1},{1,0},{2,3},{3,2},{4,5},{5,4},{6,7},{7,6},{8,9},{9,8},{10,11... | collective-permute-start | bytes 589832 | tf_op jit(solution)/shard_map/ppermute | solution.py:74
  104.2 2.1 %copy-start.13 = (f32[128,384]{1,0:T(8,128)}, f32[128,384]{1,0:T(8,128)S(1)}, u32[]{:S(2)}) copy-start(f32[128,384]{1,0:T(8,128)S(1)} %convolution_add_fusion.refs_14_) | copy-start | bytes 589828
  104.2 2.1 %copy-start.2 = (f32[128,384]{1,0:T(8,128)}, f32[128,384]{1,0:T(8,128)S(1)}, u32[]{:S(2)}) copy-start(f32[128,384]{1,0:T(8,128)S(1)} %collective-permute-done.refs_1_) | copy-start | bytes 589828
  104.2 1.5 %collective-permute-start.15 = (f32[128,384]{1,0:T(8,128)S(1)}, f32[128,384]{1,0:T(8,128)S(1)}, u32[]{:S(2)}, u32[]{:S(2)}) collective-permute-start(f32[128,384]{1,0:T(8,128)S(1)} %convolution_add_fusion.2.refs_10_), channel_id=1, source_target_pairs={{0,1},{1,0},{2,3},{3,2},{4,5},{5,4},{6,7},{7,6},{8,9},{9,8},{10,11... | collective-permute-start | bytes 589832 | tf_op jit(solution)/shard_map/ppermute | solution.py:74
  104.3 2.0 %copy-start.4 = (f32[128,384]{1,0:T(8,128)}, f32[128,384]{1,0:T(8,128)S(1)}, u32[]{:S(2)}) copy-start(f32[128,384]{1,0:T(8,128)S(1)} %collective-permute-done.3.refs_3_) | copy-start | bytes 589828
  104.3 1.7 %collective-permute-start.18 = (f32[128,384]{1,0:T(8,128)S(1)}, f32[128,384]{1,0:T(8,128)S(1)}, u32[]{:S(2)}, u32[]{:S(2)}) collective-permute-start(f32[128,384]{1,0:T(8,128)S(1)} %convolution_add_fusion.1.refs_12_), channel_id=1, source_target_pairs={{0,1},{1,0},{2,3},{3,2},{4,5},{5,4},{6,7},{7,6},{8,9},{9,8},{10,11... | collective-permute-start | bytes 589832 | tf_op jit(solution)/shard_map/ppermute | solution.py:74
  104.8 1.5 %copy-start.8 = (f32[128,384]{1,0:T(8,128)}, f32[128,384]{1,0:T(8,128)S(1)}, u32[]{:S(2)}) copy-start(f32[128,384]{1,0:T(8,128)S(1)} %collective-permute-done.6.refs_5_) | copy-start | bytes 589828
  104.8 1.5 %collective-permute-start.21 = (f32[128,384]{1,0:T(8,128)S(1)}, f32[128,384]{1,0:T(8,128)S(1)}, u32[]{:S(2)}, u32[]{:S(2)}) collective-permute-start(f32[128,384]{1,0:T(8,128)S(1)} %convolution_add_fusion.refs_14_), channel_id=1, source_target_pairs={{0,1},{1,0},{2,3},{3,2},{4,5},{5,4},{6,7},{7,6},{8,9},{9,8},{10,11... | collective-permute-start | bytes 589832 | tf_op jit(solution)/shard_map/ppermute | solution.py:74
  105.6 0.8 copy-start.11
  105.6 0.8 copy-start.12
  105.7 0.7 copy-start.14
  106.0 0.7 copy-start.15
  106.7 0.7 copy-start.16

commit v2 on v0

v2 whole, which is shorter than its diff:
```python
import functools

import jax
import jax.numpy as jnp
from jax import lax
from jax.experimental import pallas as pl
from jax.experimental.pallas import tpu as pltpu
from jax.sharding import PartitionSpec as P


NT = (((1,), (1,)), ((), ()))


def product(left, right):
    return lax.dot_general(left, right, NT, preferred_element_type=jnp.float32)


def gathered(train_grads, query_grads):
    terms = jnp.einsum(
        "lqk,nlk->qn",
        lax.all_gather(query_grads, "rows", axis=1, tiled=True),
        train_grads,
        preferred_element_type=jnp.float32,
    )
    return lax.psum_scatter(terms, "layers", scatter_dimension=0, tiled=True)


def place(sizes, half, group, plan, row_ref, *refs):
    out_ref, both_ref, sem = refs[-3:]
    row = row_ref[0]
    z, x = row // 2, row % 2
    for across, low, rows, terms in plan:
        value = None
        for array, first in terms:
            term = refs[array][first : first + rows, :]
            value = term if value is None else value + term
        at = pl.multiple_of((1 - x if across else x) * sizes + low, rows)
        both_ref[pl.ds(at, rows), :] = value
    at = pl.multiple_of(lax.rem(z - group + half, half) * 2 * sizes, 2 * sizes)
    copy = pltpu.make_async_copy(both_ref, out_ref.at[pl.ds(at, 2 * sizes), :], sem)
    copy.start()
    copy.wait()


def paired(train_grads, query_grads):
    rows, layers = lax.axis_size("rows"), lax.axis_size("layers")
    count = rows // 2
    half = count // layers
    train = train_grads.reshape(train_grads.shape[0], -1)
    queries = jnp.swapaxes(query_grads, 0, 1).reshape(query_grads.shape[1], -1)
    size, depth = queries.shape
    row, core = lax.axis_index("rows"), lax.axis_index("layers")
    z, x = row // 2, row % 2
    ring = [(2 * a + b, 2 * ((a + 1) % count) + b) for a in range(count) for b in range(2)]
    swap = [(a, a ^ 1) for a in range(rows)]

    def move(value, hops):
        return lax.ppermute(value, "rows", hops)

    def cores(value):
        return lax.ppermute(value, "layers", [(0, 1), (1, 0)])

    def columns(value, which):
        return lax.dynamic_slice_in_dim(value, which * (depth // 2), depth // 2, 1)

    cut = size // 2
    low, high = queries[:, : depth // 2], queries[:, depth // 2 :]
    held = jnp.where(x == 0, low, high)
    given = [jnp.where(x == 0, high[rows], low[rows]) for rows in (slice(0, cut), slice(cut, size))]
    firsts = {"A": held, "B": move(given[0], swap), "C": move(given[1], swap)}
    sides = {"O": columns(train, x), "N": move(columns(train, 1 - x), swap)}
    partial = {}
    for piece, value in firsts.items():
        for step in range(count):
            if step:
                value = move(value, ring)
            for side, rhs in sides.items():
                partial[side, piece, step] = product(value, rhs)

    total = None
    for group in range(half):
        mine = lax.rem(z - group + count, count) // half == core
        sums, crossed = {}, {}
        for pieces in ("A", "BC"):
            for side in "NO":
                values = [partial[side, piece, step] for step in (group, group + half) for piece in pieces]
                values = lax.optimization_barrier(values)
                one, two = [jnp.concatenate(part) for part in (values[: len(pieces)], values[len(pieces) :])]
                keep, give = jnp.where(mine, one, two), jnp.where(mine, two, one)
                sums[side] = [keep, cores(give)]
            got = move(sum(sums["N"]), swap)
            first = 0
            for piece in pieces:
                height = size if piece == "A" else cut
                for at in range(first, first + height, cut):
                    key = (piece, at - first if piece == "A" else 0)
                    crossed[key] = (got, at)
                    sums[key] = [(value, at) for value in sums["O"]]
                first += height
        plan = []
        operands = []

        def index_of(value):
            for i, other in enumerate(operands):
                if other is value:
                    return i
            operands.append(value)
            return len(operands) - 1

        for mine_key, their_key, across, at in (
            (("A", 0), ("B", 0), False, 0),
            (("A", cut), ("C", 0), False, cut),
            (("B", 0), ("A", 0), True, 0),
            (("C", 0), ("A", cut), True, cut),
        ):
            terms = [*sums[mine_key], crossed[their_key]]
            plan.append((across, at, cut, [(index_of(value), first) for value, first in terms]))
        specs = [pl.BlockSpec(memory_space=pltpu.SMEM)] + [pl.BlockSpec(memory_space=pltpu.VMEM)] * len(operands)
        aliases = {}
        if total is not None:
            aliases = {len(operands) + 1: 0}
            operands.append(total)
            specs.append(pl.BlockSpec(memory_space=pl.ANY))
        total = pl.pallas_call(
            functools.partial(place, size, half, group, plan),
            out_shape=jax.ShapeDtypeStruct((rows * size // layers, train.shape[0]), jnp.float32),
            in_specs=specs,
            out_specs=pl.BlockSpec(memory_space=pl.ANY),
            scratch_shapes=[pltpu.VMEM((2 * size, train.shape[0]), jnp.float32), pltpu.SemaphoreType.DMA],
            input_output_aliases=aliases,
            compiler_params=pltpu.CompilerParams(vmem_limit_bytes=8 * 2**20),
        )(row.astype(jnp.int32).reshape(1), *operands)
    return total


def solution(mesh):
    in_specs = (P(("groups", "rows"), "layers", None), P("layers", ("groups", "rows"), None))
    out_specs = P("layers", ("groups", "rows"))
    special = mesh.shape["rows"] == 8 and mesh.shape["layers"] == 2
    shards = paired if special else gathered
    return jax.shard_map(shards, mesh=mesh, in_specs=in_specs, out_specs=out_specs, check_vma=False)
```

time: 159 us -> 166 us (1.044)
  waiting for transfers between devices: 137 us -> 98.8 us
  matrix products: 8.13 us -> 35.4 us
  starting transfers between devices: 0.04 us -> 21.9 us
  between operations: 13.4 us -> 0.54 us
  local copies, waits for them, and re-layouts: 0.01 us -> 3.36 us
  other arithmetic: 0 us -> 3.31 us
    all_gather x1 -> x0, waiting for transfers between devices: 129 us -> none  [shards(): lax.all_gather(query_grads, 'rows', axis=1, tiled=True)]
    ppermute x0 -> x24, waiting for transfers between devices: none -> 98.8 us  [the longest x16 98 us: move(): return lax.ppermute(value, 'rows', hops)]
    dot_general x1 -> x24, matrix products: 8.13 us -> 35.4 us  [product(): return lax.dot_general(left, right, NT, preferred_element_type=jnp.float32)]
    ppermute x0 -> x24, starting transfers between devices: none -> 21.9 us  [the longest x16 20.3 us: move(): return lax.ppermute(value, 'rows', hops)]
    reduce_scatter x1 -> x0, waiting for transfers between devices: 7.37 us -> none  [shards(): return lax.psum_scatter(terms, 'layers', scatter_dimension=0, tiled=True)]
    select_n x0 -> x10, other arithmetic: none -> 3.19 us  [the longest x1 2.12 us: paired(): jnp.where(x == 0, high[rows], low[rows])]
    unnamed x2 -> x14, local copies, waits for them, and re-layouts: 0.01 us -> 1.96 us
    pallas_call x0 -> x2, Pallas kernels: none -> 1.66 us  [paired(): pl.pallas_call(functools.partial(place, size, half, group, plan), out_sha...]
  transfers between devices with their start and end apart: 2 -> 24, of which waited for: 2 -> 13; matrix products, arithmetic and copies ran while one was open for 0% -> 24% of each run, Pallas kernels for 0% -> 1%
where the time goes in v2:
time: 166 us; the launch traced here: 165 us
  waiting for transfers between devices  98.8 us (60%)
  matrix products  35.4 us (21%)
  starting transfers between devices  21.9 us (13%)
  local copies, waits for them, and re-layouts  3.36 us (2%)
  other arithmetic  3.31 us (2%)
    ppermute x16, waiting for transfers between devices, move(): return lax.ppermute(value, 'rows', hops)  98 us
    dot_general x24, matrix products, product(): return lax.dot_general(left, right, NT, preferred_element_type=jnp.float32)  35.4 us
    ppermute x16, starting transfers between devices, move(): return lax.ppermute(value, 'rows', hops)  20.3 us
  transfers between devices with their start and end apart: 24, of which 13 were waited for; matrix products, arithmetic and copies ran while one was open for 24% of the time, Pallas kernels for 1%

profile of v2, /device:TPU:0, one launch (start us, length us, event | category | flops | bytes accessed | tf_op | source)
XLA Modules:
  0.0 164.9 jit_solution(15727171427942099939)
XLA Ops:
  0.0 1.9 %copy-done = bf16[384,1,4096]{2,0,1:T(8,128)(2,1)S(1)} copy-done((bf16[384,1,4096]{2,0,1:T(8,128)(2,1)S(1)}, bf16[384,1,4096]{2,0,1:T(8,128)(2,1)}, u32[]{:S(2)}) %copy-start) | copy-done | bytes 3145752
  1.9 1.3 dynamic-slice_bitcast_fusion
  3.2 3.0 %collective-permute-start.6 = (bf16[384,2048]{1,0:T(8,128)(2,1)}, bf16[384,2048]{1,0:T(8,128)(2,1)}, u32[]{:S(2)}, u32[]{:S(2)}) collective-permute-start(bf16[384,2048]{1,0:T(8,128)(2,1)} %dynamic-slice_bitcast_fusion), channel_id=1, source_target_pairs={{0,2},{2,0},{4,6},{6,4},{8,10},{10,8},{12,14},{14,12},{1,3},{3,1},... | collective-permute-start | bytes 4718600 | tf_op jit(solution)/shard_map/ppermute | solution.py:58
  6.2 2.1 %slice_select_fusion.1 = (bf16[64,2048]{1,0:T(8,128)(2,1)}, bf16[64,2048]{1,0:T(8,128)(2,1)}) fusion(bf16[128,4096]{1,0:T(8,128)(2,1)} %bitcast.65, pred[]{:T(512)S(6)} %eq.14), kind=kLoop, calls=%fused_computation.26 | loop fusion | flops 262144 | bytes 1572865 | tf_op jit(solution)/shard_map/jit(_where)/select_n | solution.py:69
  8.3 2.0 %collective-permute-start.4 = (bf16[64,2048]{1,0:T(8,128)(2,1)}, bf16[64,2048]{1,0:T(8,128)(2,1)}, u32[]{:S(2)}, u32[]{:S(2)}) collective-permute-start(bf16[64,2048]{1,0:T(8,128)(2,1)} %get-tuple-element.54), channel_id=1, source_target_pairs={{0,2},{2,0},{4,6},{6,4},{8,10},{10,8},{12,14},{14,12},{1,3},{3,1},... | collective-permute-start | bytes 786440 | tf_op jit(solution)/shard_map/ppermute | solution.py:58
  10.3 0.8 slice_select_fusion
  11.2 1.6 collective-permute-start
  12.8 2.4 %fusion.10 = f32[128,384]{1,0:T(8,128)} fusion(bf16[128,2048]{1,0:T(8,128)(2,1)} %slice_select_fusion, bf16[384,1,4096]{2,0,1:T(8,128)(2,1)S(1)} %copy-done, s32[]{:T(128)S(6)} %select_n.119), kind=kOutput, calls=%fused_computation.10 | convolution fusion | flops 201326592 | bytes 2293764 | tf_op jit(solution)/shard_map/dot_general | solution.py:15
  15.1 32.1 %collective-permute-done.7 = bf16[64,2048]{1,0:T(8,128)(2,1)S(1)} collective-permute-done((bf16[64,2048]{1,0:T(8,128)(2,1)}, bf16[64,2048]{1,0:T(8,128)(2,1)S(1)}, u32[]{:S(2)}, u32[]{:S(2)}) %collective-permute-start.7) | collective-permute-done | bytes 262176 | tf_op jit(solution)/shard_map/ppermute | solution.py:58
  47.3 2.1 %collective-permute-start.8 = (bf16[64,2048]{1,0:T(8,128)(2,1)S(1)}, bf16[64,2048]{1,0:T(8,128)(2,1)S(1)}, u32[]{:S(2)}, u32[]{:S(2)}) collective-permute-start(bf16[64,2048]{1,0:T(8,128)(2,1)S(1)} %collective-permute-done.7), channel_id=1, source_target_pairs={{0,4},{2,6},{4,8},{6,10},{8,12},{10,14},{12,0},{14,2},{1,5},{3,7},... | collective-permute-start | bytes 786440 | tf_op jit(solution)/shard_map/ppermute | solution.py:58
  49.4 2.8 %collective-permute-done.4 = bf16[64,2048]{1,0:T(8,128)(2,1)} collective-permute-done((bf16[64,2048]{1,0:T(8,128)(2,1)}, bf16[64,2048]{1,0:T(8,128)(2,1)}, u32[]{:S(2)}, u32[]{:S(2)}) %collective-permute-start.4) | collective-permute-done | bytes 262176 | tf_op jit(solution)/shard_map/ppermute | solution.py:58
  52.1 1.8 %collective-permute-start.5 = (bf16[64,2048]{1,0:T(8,128)(2,1)}, bf16[64,2048]{1,0:T(8,128)(2,1)S(1)}, u32[]{:S(2)}, u32[]{:S(2)}) collective-permute-start(bf16[64,2048]{1,0:T(8,128)(2,1)} %collective-permute-done.4), channel_id=1, source_target_pairs={{0,4},{2,6},{4,8},{6,10},{8,12},{10,14},{12,0},{14,2},{1,5},{3,7},... | collective-permute-start | bytes 786440 | tf_op jit(solution)/shard_map/ppermute | solution.py:58
  54.6 1.6 fusion.6
  56.1 1.6 collective-permute-start.1
  57.8 1.7 %fusion.22 = f32[128,384]{1,0:T(8,128)S(1)} fusion(bf16[128,2048]{1,0:T(8,128)(2,1)} %collective-permute-done, bf16[384,1,4096]{2,0,1:T(8,128)(2,1)S(1)} %copy-done, s32[]{:T(128)S(6)} %select_n.119), kind=kOutput, calls=%fused_computation.22 | convolution fusion | flops 201326592 | bytes 2293764 | tf_op jit(solution)/shard_map/dot_general | solution.py:15
  59.4 1.6 collective-permute-start.11
  61.7 1.7 %collective-permute-done.5 = bf16[64,2048]{1,0:T(8,128)(2,1)S(1)} collective-permute-done((bf16[64,2048]{1,0:T(8,128)(2,1)}, bf16[64,2048]{1,0:T(8,128)(2,1)S(1)}, u32[]{:S(2)}, u32[]{:S(2)}) %collective-permute-start.5) | collective-permute-done | bytes 262176 | tf_op jit(solution)/shard_map/ppermute | solution.py:58
  63.3 0.6 fusion.18
  64.0 16.2 %collective-permute-done.11 = bf16[64,2048]{1,0:T(8,128)(2,1)S(1)} collective-permute-done((bf16[64,2048]{1,0:T(8,128)(2,1)S(1)}, bf16[64,2048]{1,0:T(8,128)(2,1)S(1)}, u32[]{:S(2)}, u32[]{:S(2)}) %collective-permute-start.11) | collective-permute-done | bytes 262176 | tf_op jit(solution)/shard_map/ppermute | solution.py:58
  80.2 0.6 fusion
  80.8 3.3 %collective-permute-done.9 = bf16[64,2048]{1,0:T(8,128)(2,1)S(1)} collective-permute-done((bf16[64,2048]{1,0:T(8,128)(2,1)S(1)}, bf16[64,2048]{1,0:T(8,128)(2,1)S(1)}, u32[]{:S(2)}, u32[]{:S(2)}) %collective-permute-start.9) | collective-permute-done | bytes 262176 | tf_op jit(solution)/shard_map/ppermute | solution.py:58
  85.0 1.3 collective-permute-start.10
  87.0 8.9 %collective-permute-done.12 = bf16[64,2048]{1,0:T(8,128)(2,1)S(1)} collective-permute-done((bf16[64,2048]{1,0:T(8,128)(2,1)S(1)}, bf16[64,2048]{1,0:T(8,128)(2,1)S(1)}, u32[]{:S(2)}, u32[]{:S(2)}) %collective-permute-start.12) | collective-permute-done | bytes 262176 | tf_op jit(solution)/shard_map/ppermute | solution.py:58
  96.5 4.5 %collective-permute-done.10 = bf16[64,2048]{1,0:T(8,128)(2,1)S(1)} collective-permute-done((bf16[64,2048]{1,0:T(8,128)(2,1)S(1)}, bf16[64,2048]{1,0:T(8,128)(2,1)S(1)}, u32[]{:S(2)}, u32[]{:S(2)}) %collective-permute-start.10) | collective-permute-done | bytes 262176 | tf_op jit(solution)/shard_map/ppermute | solution.py:58
  101.9 15.0 %collective-permute-done.2 = bf16[128,2048]{1,0:T(8,128)(2,1)S(1)} collective-permute-done((bf16[128,2048]{1,0:T(8,128)(2,1)S(1)}, bf16[128,2048]{1,0:T(8,128)(2,1)S(1)}, u32[]{:S(2)}, u32[]{:S(2)}) %collective-permute-start.2) | collective-permute-done | bytes 524320 | tf_op jit(solution)/shard_map/ppermute | solution.py:58
  117.6 2.0 %fusion.35 = f32[128,384]{1,0:T(8,128)S(1)} fusion(bf16[128,2048]{1,0:T(8,128)(2,1)S(1)} %collective-permute-done.1, bf16[384,2048]{1,0:T(8,128)(2,1)} %collective-permute-done.6), kind=kOutput, calls=%fused_computation.72 | convolution fusion | flops 201326592 | bytes 2293760 | tf_op jit(solution)/shard_map/dot_general | solution.py:15
  119.6 2.2 %fusion.34 = f32[128,384]{1,0:T(8,128)S(1)} fusion(bf16[128,2048]{1,0:T(8,128)(2,1)} %slice_select_fusion, bf16[384,2048]{1,0:T(8,128)(2,1)} %collective-permute-done.6), kind=kOutput, calls=%fused_computation.71 | convolution fusion | flops 201326592 | bytes 2293760 | tf_op jit(solution)/shard_map/dot_general | solution.py:15
  121.9 2.0 %fusion.32 = f32[64,384]{1,0:T(8,128)S(1)} fusion(bf16[64,2048]{1,0:T(8,128)(2,1)S(1)} %collective-permute-done.9, bf16[384,2048]{1,0:T(8,128)(2,1)} %collective-permute-done.6), kind=kOutput, calls=%fused_computation.69 | convolution fusion | flops 100663296 | bytes 1933312 | tf_op jit(solution)/shard_map/dot_general | solution.py:15
  123.9 2.0 %fusion.33 = f32[64,384]{1,0:T(8,128)S(1)} fusion(bf16[64,2048]{1,0:T(8,128)(2,1)S(1)} %collective-permute-done.11, bf16[384,2048]{1,0:T(8,128)(2,1)} %collective-permute-done.6), kind=kOutput, calls=%fused_computation.70 | convolution fusion | flops 100663296 | bytes 1933312 | tf_op jit(solution)/shard_map/dot_general | solution.py:15
  125.9 2.1 %fusion.30 = f32[64,384]{1,0:T(8,128)S(1)} fusion(bf16[64,2048]{1,0:T(8,128)(2,1)} %collective-permute-done.4, bf16[384,2048]{1,0:T(8,128)(2,1)} %collective-permute-done.6), kind=kOutput, calls=%fused_computation.67 | convolution fusion | flops 100663296 | bytes 1933312 | tf_op jit(solution)/shard_map/dot_general | solution.py:15
  128.0 2.0 %fusion.31 = f32[64,384]{1,0:T(8,128)S(1)} fusion(bf16[64,2048]{1,0:T(8,128)(2,1)S(1)} %collective-permute-done.7, bf16[384,2048]{1,0:T(8,128)(2,1)} %collective-permute-done.6), kind=kOutput, calls=%fused_computation.68 | convolution fusion | flops 100663296 | bytes 1933312 | tf_op jit(solution)/shard_map/dot_general | solution.py:15
  130.7 2.0 %fusion.29 = f32[128,384]{1,0:T(8,128)S(1)} fusion(bf16[128,2048]{1,0:T(8,128)(2,1)S(1)} %collective-permute-done.2, bf16[384,2048]{1,0:T(8,128)(2,1)} %collective-permute-done.6), kind=kOutput, calls=%fused_computation.66 | convolution fusion | flops 201326592 | bytes 2293760 | tf_op jit(solution)/shard_map/dot_general | solution.py:15
  132.7 2.2 %fusion.28 = f32[128,384]{1,0:T(8,128)S(1)} fusion(bf16[128,2048]{1,0:T(8,128)(2,1)} %collective-permute-done, bf16[384,2048]{1,0:T(8,128)(2,1)} %collective-permute-done.6), kind=kOutput, calls=%fused_computation.65 | convolution fusion | flops 201326592 | bytes 2293760 | tf_op jit(solution)/shard_map/dot_general | solution.py:15
  134.8 2.0 %fusion.26 = f32[64,384]{1,0:T(8,128)S(1)} fusion(bf16[64,2048]{1,0:T(8,128)(2,1)S(1)} %collective-permute-done.10, bf16[384,2048]{1,0:T(8,128)(2,1)} %collective-permute-done.6), kind=kOutput, calls=%fused_computation.63 | convolution fusion | flops 100663296 | bytes 1933312 | tf_op jit(solution)/shard_map/dot_general | solution.py:15
  136.9 2.0 %fusion.27 = f32[64,384]{1,0:T(8,128)S(1)} fusion(bf16[64,2048]{1,0:T(8,128)(2,1)S(1)} %collective-permute-done.12, bf16[384,2048]{1,0:T(8,128)(2,1)} %collective-permute-done.6), kind=kOutput, calls=%fused_computation.64 | convolution fusion | flops 100663296 | bytes 1933312 | tf_op jit(solution)/shard_map/dot_general | solution.py:15
  138.9 2.0 %fusion.24 = f32[64,384]{1,0:T(8,128)S(1)} fusion(bf16[64,2048]{1,0:T(8,128)(2,1)S(1)} %collective-permute-done.5, bf16[384,2048]{1,0:T(8,128)(2,1)} %collective-permute-done.6), kind=kOutput, calls=%fused_computation.61 | convolution fusion | flops 100663296 | bytes 1933312 | tf_op jit(solution)/shard_map/dot_general | solution.py:15
  140.9 2.0 %fusion.25 = f32[64,384]{1,0:T(8,128)S(1)} fusion(bf16[64,2048]{1,0:T(8,128)(2,1)S(1)} %collective-permute-done.8, bf16[384,2048]{1,0:T(8,128)(2,1)} %collective-permute-done.6), kind=kOutput, calls=%fused_computation.62 | convolution fusion | flops 100663296 | bytes 1933312 | tf_op jit(solution)/shard_map/dot_general | solution.py:15
  143.7 0.8 collective-permute-done.16
  144.5 1.5 collective-permute-start.23
  146.1 0.6 collective-permute-start.20
  146.8 1.6 collective-permute-start.17
  148.4 3.9 %collective-permute-done.23.refs_5_ = f32[128,384]{1,0:T(8,128)S(1)} collective-permute-done((f32[128,384]{1,0:T(8,128)S(1)}, f32[128,384]{1,0:T(8,128)S(1)}, u32[]{:S(2)}, u32[]{:S(2)}) %collective-permute-start.23) | collective-permute-done | bytes 196640 | tf_op jit(solution)/shard_map/ppermute | solution.py:58
  152.3 1.5 collective-permute-start.14
  153.8 2.7 %collective-permute-done.20.refs_2_ = f32[128,384]{1,0:T(8,128)S(1)} collective-permute-done((f32[128,384]{1,0:T(8,128)S(1)}, f32[128,384]{1,0:T(8,128)S(1)}, u32[]{:S(2)}, u32[]{:S(2)}) %collective-permute-start.20) | collective-permute-done | bytes 196640 | tf_op jit(solution)/shard_map/ppermute | solution.py:58
  156.5 0.9 shard_map.28.refs_6_
  157.4 3.3 %collective-permute-done.17.refs_5_ = f32[128,384]{1,0:T(8,128)S(1)} collective-permute-done((f32[128,384]{1,0:T(8,128)S(1)}, f32[128,384]{1,0:T(8,128)S(1)}, u32[]{:S(2)}, u32[]{:S(2)}) %collective-permute-start.17) | collective-permute-done | bytes 196640 | tf_op jit(solution)/shard_map/ppermute | solution.py:58
  160.7 3.4 %collective-permute-done.14.refs_2_ = f32[128,384]{1,0:T(8,128)S(1)} collective-permute-done((f32[128,384]{1,0:T(8,128)S(1)}, f32[128,384]{1,0:T(8,128)S(1)}, u32[]{:S(2)}, u32[]{:S(2)}) %collective-permute-start.14) | collective-permute-done | bytes 196640 | tf_op jit(solution)/shard_map/ppermute | solution.py:58
  164.1 0.8 shard_map.29
  (59 shorter events, 6.4 us)
Async XLA Ops:
  0.0 1.9 %copy-start = (bf16[384,1,4096]{2,0,1:T(8,128)(2,1)S(1)}, bf16[384,1,4096]{2,0,1:T(8,128)(2,1)}, u32[]{:S(2)}) copy-start(bf16[384,1,4096]{2,0,1:T(8,128)(2,1)} %param.2) | copy-start | bytes 9437188
  3.2 114.3 %collective-permute-start.6 = (bf16[384,2048]{1,0:T(8,128)(2,1)}, bf16[384,2048]{1,0:T(8,128)(2,1)}, u32[]{:S(2)}, u32[]{:S(2)}) collective-permute-start(bf16[384,2048]{1,0:T(8,128)(2,1)} %dynamic-slice_bitcast_fusion), channel_id=1, source_target_pairs={{0,2},{2,0},{4,6},{6,4},{8,10},{10,8},{12,14},{14,12},{1,3},{3,1},... | collective-permute-start | bytes 4718600 | tf_op jit(solution)/shard_map/ppermute | solution.py:58
  6.2 4.2 %copy-start.1 = (bf16[1,128,4096]{2,1,0:T(8,128)(2,1)S(1)}, bf16[1,128,4096]{2,1,0:T(8,128)(2,1)}, u32[]{:S(2)}) copy-start(bf16[1,128,4096]{2,1,0:T(8,128)(2,1)} %param.3) | copy-start | bytes 3145732
  8.3 38.9 %collective-permute-start.7 = (bf16[64,2048]{1,0:T(8,128)(2,1)}, bf16[64,2048]{1,0:T(8,128)(2,1)S(1)}, u32[]{:S(2)}, u32[]{:S(2)}) collective-permute-start(bf16[64,2048]{1,0:T(8,128)(2,1)} %get-tuple-element.53), channel_id=1, source_target_pairs={{0,2},{2,0},{4,6},{6,4},{8,10},{10,8},{12,14},{14,12},{1,3},{3,1},... | collective-permute-start | bytes 786440 | tf_op jit(solution)/shard_map/ppermute | solution.py:58
  8.3 43.8 %collective-permute-start.4 = (bf16[64,2048]{1,0:T(8,128)(2,1)}, bf16[64,2048]{1,0:T(8,128)(2,1)}, u32[]{:S(2)}, u32[]{:S(2)}) collective-permute-start(bf16[64,2048]{1,0:T(8,128)(2,1)} %get-tuple-element.54), channel_id=1, source_target_pairs={{0,2},{2,0},{4,6},{6,4},{8,10},{10,8},{12,14},{14,12},{1,3},{3,1},... | collective-permute-start | bytes 786440 | tf_op jit(solution)/shard_map/ppermute | solution.py:58
  11.2 44.9 %collective-permute-start = (bf16[128,2048]{1,0:T(8,128)(2,1)}, bf16[128,2048]{1,0:T(8,128)(2,1)}, u32[]{:S(2)}, u32[]{:S(2)}) collective-permute-start(bf16[128,2048]{1,0:T(8,128)(2,1)} %slice_select_fusion), channel_id=1, source_target_pairs={{0,4},{2,6},{4,8},{6,10},{8,12},{10,14},{12,0},{14,2},{1,5},{3,7},... | collective-permute-start | bytes 1572872 | tf_op jit(solution)/shard_map/ppermute | solution.py:58
  47.3 12.2 %collective-permute-start.8 = (bf16[64,2048]{1,0:T(8,128)(2,1)S(1)}, bf16[64,2048]{1,0:T(8,128)(2,1)S(1)}, u32[]{:S(2)}, u32[]{:S(2)}) collective-permute-start(bf16[64,2048]{1,0:T(8,128)(2,1)S(1)} %collective-permute-done.7), channel_id=1, source_target_pairs={{0,4},{2,6},{4,8},{6,10},{8,12},{10,14},{12,0},{14,2},{1,5},{3,7},... | collective-permute-start | bytes 786440 | tf_op jit(solution)/shard_map/ppermute | solution.py:58
  52.1 11.2 %collective-permute-start.5 = (bf16[64,2048]{1,0:T(8,128)(2,1)}, bf16[64,2048]{1,0:T(8,128)(2,1)S(1)}, u32[]{:S(2)}, u32[]{:S(2)}) collective-permute-start(bf16[64,2048]{1,0:T(8,128)(2,1)} %collective-permute-done.4), channel_id=1, source_target_pairs={{0,4},{2,6},{4,8},{6,10},{8,12},{10,14},{12,0},{14,2},{1,5},{3,7},... | collective-permute-start | bytes 786440 | tf_op jit(solution)/shard_map/ppermute | solution.py:58
  56.1 30.1 %collective-permute-start.1 = (bf16[128,2048]{1,0:T(8,128)(2,1)}, bf16[128,2048]{1,0:T(8,128)(2,1)S(1)}, u32[]{:S(2)}, u32[]{:S(2)}) collective-permute-start(bf16[128,2048]{1,0:T(8,128)(2,1)} %collective-permute-done), channel_id=1, source_target_pairs={{0,4},{2,6},{4,8},{6,10},{8,12},{10,14},{12,0},{14,2},{1,5},{3,7},... | collective-permute-start | bytes 1572872 | tf_op jit(solution)/shard_map/ppermute | solution.py:58
  59.4 20.8 %collective-permute-start.11 = (bf16[64,2048]{1,0:T(8,128)(2,1)S(1)}, bf16[64,2048]{1,0:T(8,128)(2,1)S(1)}, u32[]{:S(2)}, u32[]{:S(2)}) collective-permute-start(bf16[64,2048]{1,0:T(8,128)(2,1)S(1)} %collective-permute-done.8), channel_id=1, source_target_pairs={{0,4},{2,6},{4,8},{6,10},{8,12},{10,14},{12,0},{14,2},{1,5},{3,7},... | collective-permute-start | bytes 786440 | tf_op jit(solution)/shard_map/ppermute | solution.py:58
  63.3 20.8 %collective-permute-start.9 = (bf16[64,2048]{1,0:T(8,128)(2,1)S(1)}, bf16[64,2048]{1,0:T(8,128)(2,1)S(1)}, u32[]{:S(2)}, u32[]{:S(2)}) collective-permute-start(bf16[64,2048]{1,0:T(8,128)(2,1)S(1)} %collective-permute-done.5), channel_id=1, source_target_pairs={{0,4},{2,6},{4,8},{6,10},{8,12},{10,14},{12,0},{14,2},{1,5},{3,7},... | collective-permute-start | bytes 786440 | tf_op jit(solution)/shard_map/ppermute | solution.py:58
  84.8 2.1 %copy-start.2 = (f32[128,384]{1,0:T(8,128)S(1)}, f32[128,384]{1,0:T(8,128)}, u32[]{:S(2)}) copy-start(f32[128,384]{1,0:T(8,128)} %fusion.10) | copy-start | bytes 589828
  84.8 61.9 %collective-permute-start.21 = (f32[128,384]{1,0:T(8,128)S(1)}, f32[128,384]{1,0:T(8,128)S(1)}, u32[]{:S(2)}, u32[]{:S(2)}) collective-permute-start(f32[128,384]{1,0:T(8,128)S(1)} %get-tuple-element.55), channel_id=1, source_target_pairs={{0,1},{1,0},{2,3},{3,2},{4,5},{5,4},{6,7},{7,6},{8,9},{9,8},{10,11... | collective-permute-start | bytes 589832 | tf_op jit(solution)/shard_map/ppermute | solution.py:61
  84.9 11.0 %collective-permute-start.12 = (bf16[64,2048]{1,0:T(8,128)(2,1)S(1)}, bf16[64,2048]{1,0:T(8,128)(2,1)S(1)}, u32[]{:S(2)}, u32[]{:S(2)}) collective-permute-start(bf16[64,2048]{1,0:T(8,128)(2,1)S(1)} %collective-permute-done.11), channel_id=1, source_target_pairs={{0,4},{2,6},{4,8},{6,10},{8,12},{10,14},{12,0},{14,2},{1,5},{3,7},... | collective-permute-start | bytes 786440 | tf_op jit(solution)/shard_map/ppermute | solution.py:58
  85.0 16.1 %collective-permute-start.10 = (bf16[64,2048]{1,0:T(8,128)(2,1)S(1)}, bf16[64,2048]{1,0:T(8,128)(2,1)S(1)}, u32[]{:S(2)}, u32[]{:S(2)}) collective-permute-start(bf16[64,2048]{1,0:T(8,128)(2,1)S(1)} %collective-permute-done.9), channel_id=1, source_target_pairs={{0,4},{2,6},{4,8},{6,10},{8,12},{10,14},{12,0},{14,2},{1,5},{3,7},... | collective-permute-start | bytes 786440 | tf_op jit(solution)/shard_map/ppermute | solution.py:58
  86.9 59.9 %collective-permute-start.18 = (f32[128,384]{1,0:T(8,128)S(1)}, f32[128,384]{1,0:T(8,128)S(1)}, u32[]{:S(2)}, u32[]{:S(2)}) collective-permute-start(f32[128,384]{1,0:T(8,128)S(1)} %get-tuple-element.57), channel_id=1, source_target_pairs={{0,1},{1,0},{2,3},{3,2},{4,5},{5,4},{6,7},{7,6},{8,9},{9,8},{10,11... | collective-permute-start | bytes 589832 | tf_op jit(solution)/shard_map/ppermute | solution.py:61
  101.6 15.3 %collective-permute-start.2 = (bf16[128,2048]{1,0:T(8,128)(2,1)S(1)}, bf16[128,2048]{1,0:T(8,128)(2,1)S(1)}, u32[]{:S(2)}, u32[]{:S(2)}) collective-permute-start(bf16[128,2048]{1,0:T(8,128)(2,1)S(1)} %collective-permute-done.1), channel_id=1, source_target_pairs={{0,4},{2,6},{4,8},{6,10},{8,12},{10,14},{12,0},{14,2},{1,5},{3,7},... | collective-permute-start | bytes 1572872 | tf_op jit(solution)/shard_map/ppermute | solution.py:58
  101.8 55.6 %collective-permute-start.15 = (f32[128,384]{1,0:T(8,128)S(1)}, f32[128,384]{1,0:T(8,128)S(1)}, u32[]{:S(2)}, u32[]{:S(2)}) collective-permute-start(f32[128,384]{1,0:T(8,128)S(1)} %get-tuple-element.59), channel_id=1, source_target_pairs={{0,1},{1,0},{2,3},{3,2},{4,5},{5,4},{6,7},{7,6},{8,9},{9,8},{10,11... | collective-permute-start | bytes 589832 | tf_op jit(solution)/shard_map/ppermute | solution.py:61
  121.8 21.2 %collective-permute-start.22 = (f32[128,384]{1,0:T(8,128)S(1)}, f32[128,384]{1,0:T(8,128)S(1)}, u32[]{:S(2)}, u32[]{:S(2)}) collective-permute-start(f32[128,384]{1,0:T(8,128)S(1)} %broadcast_select_fusion), channel_id=1, source_target_pairs={{0,1},{1,0},{2,3},{3,2},{4,5},{5,4},{6,7},{7,6},{8,9},{9,8},{10,11... | collective-permute-start | bytes 589832 | tf_op jit(solution)/shard_map/ppermute | solution.py:61
  130.1 13.1 %collective-permute-start.19 = (f32[128,384]{1,0:T(8,128)S(1)}, f32[128,384]{1,0:T(8,128)S(1)}, u32[]{:S(2)}, u32[]{:S(2)}) collective-permute-start(f32[128,384]{1,0:T(8,128)S(1)} %broadcast_select_fusion.3), channel_id=1, source_target_pairs={{0,1},{1,0},{2,3},{3,2},{4,5},{5,4},{6,7},{7,6},{8,9},{9,8},{10,11... | collective-permute-start | bytes 589832 | tf_op jit(solution)/shard_map/ppermute | solution.py:61
  143.0 1.5 collective-permute-start.16
  143.2 2.9 %collective-permute-start.13 = (f32[128,384]{1,0:T(8,128)S(1)}, f32[128,384]{1,0:T(8,128)S(1)}, u32[]{:S(2)}, u32[]{:S(2)}) collective-permute-start(f32[128,384]{1,0:T(8,128)S(1)} %broadcast_select_fusion.9), channel_id=1, source_target_pairs={{0,1},{1,0},{2,3},{3,2},{4,5},{5,4},{6,7},{7,6},{8,9},{9,8},{10,11... | collective-permute-start | bytes 589832 | tf_op jit(solution)/shard_map/ppermute | solution.py:61
  144.5 7.8 %collective-permute-start.23 = (f32[128,384]{1,0:T(8,128)S(1)}, f32[128,384]{1,0:T(8,128)S(1)}, u32[]{:S(2)}, u32[]{:S(2)}) collective-permute-start(f32[128,384]{1,0:T(8,128)S(1)} %select_add_fusion), channel_id=1, source_target_pairs={{0,2},{2,0},{4,6},{6,4},{8,10},{10,8},{12,14},{14,12},{1,3},{3,1},... | collective-permute-start | bytes 589832 | tf_op jit(solution)/shard_map/ppermute | solution.py:58
  146.1 10.5 %collective-permute-start.20 = (f32[128,384]{1,0:T(8,128)S(1)}, f32[128,384]{1,0:T(8,128)S(1)}, u32[]{:S(2)}, u32[]{:S(2)}) collective-permute-start(f32[128,384]{1,0:T(8,128)S(1)} %select_add_fusion.1), channel_id=1, source_target_pairs={{0,2},{2,0},{4,6},{6,4},{8,10},{10,8},{12,14},{14,12},{1,3},{3,1},... | collective-permute-start | bytes 589832 | tf_op jit(solution)/shard_map/ppermute | solution.py:58
  146.7 10.7 %collective-permute-start.3 = (f32[128,384]{1,0:T(8,128)S(1)}, f32[128,384]{1,0:T(8,128)S(1)}, u32[]{:S(2)}, u32[]{:S(2)}) collective-permute-start(f32[128,384]{1,0:T(8,128)S(1)} %get-tuple-element.61), channel_id=1, source_target_pairs={{0,1},{1,0},{2,3},{3,2},{4,5},{5,4},{6,7},{7,6},{8,9},{9,8},{10,11... | collective-permute-start | bytes 589832 | tf_op jit(solution)/shard_map/ppermute | solution.py:61
  146.8 13.9 %collective-permute-start.17 = (f32[128,384]{1,0:T(8,128)S(1)}, f32[128,384]{1,0:T(8,128)S(1)}, u32[]{:S(2)}, u32[]{:S(2)}) collective-permute-start(f32[128,384]{1,0:T(8,128)S(1)} %select_add_fusion.2), channel_id=1, source_target_pairs={{0,2},{2,0},{4,6},{6,4},{8,10},{10,8},{12,14},{14,12},{1,3},{3,1},... | collective-permute-start | bytes 589832 | tf_op jit(solution)/shard_map/ppermute | solution.py:58
  152.3 11.8 %collective-permute-start.14 = (f32[128,384]{1,0:T(8,128)S(1)}, f32[128,384]{1,0:T(8,128)S(1)}, u32[]{:S(2)}, u32[]{:S(2)}) collective-permute-start(f32[128,384]{1,0:T(8,128)S(1)} %select_add_fusion.3), channel_id=1, source_target_pairs={{0,2},{2,0},{4,6},{6,4},{8,10},{10,8},{12,14},{14,12},{1,3},{3,1},... | collective-permute-start | bytes 589832 | tf_op jit(solution)/shard_map/ppermute | solution.py:58

commit v3 on v2

--- a/solution.py
+++ b/solution.py
@@ -1,4 +1,5 @@
 import functools
+import math
 
 import jax
 import jax.numpy as jnp
@@ -34,12 +35,41 @@
         for array, first in terms:
             term = refs[array][first : first + rows, :]
             value = term if value is None else value + term
-        at = pl.multiple_of((1 - x if across else x) * sizes + low, rows)
+        at = pl.multiple_of((1 - x if across else x) * sizes + low, math.gcd(sizes, low))
         both_ref[pl.ds(at, rows), :] = value
-    at = pl.multiple_of(lax.rem(z - group + half, half) * 2 * sizes, 2 * sizes)
+    at = pl.multiple_of(lax.rem(z + group, half) * 2 * sizes, 2 * sizes)
     copy = pltpu.make_async_copy(both_ref, out_ref.at[pl.ds(at, 2 * sizes), :], sem)
     copy.start()
     copy.wait()
+
+
+def part(cut, row_ref, queries_ref, held_ref, b_ref, c_ref, sems):
+    half = held_ref.shape[1]
+    x = row_ref[0] % 2
+    mine, other = (pl.ds(pl.multiple_of(side * half, half), half) for side in (x, 1 - x))
+    copies = [
+        pltpu.make_async_copy(queries_ref.at[:, mine], held_ref, sems.at[0]),
+        pltpu.make_async_copy(queries_ref.at[:cut, other], b_ref, sems.at[1]),
+        pltpu.make_async_copy(queries_ref.at[cut:, other], c_ref, sems.at[2]),
+    ]
+    for copy in copies:
+        copy.start()
+    for copy in copies:
+        copy.wait()
+
+
+def parted(row, queries, cut):
+    size, depth = queries.shape
+    shapes = [(size, depth // 2), (cut, depth // 2), (size - cut, depth // 2)]
+    return pl.pallas_call(
+        functools.partial(part, cut),
+        out_shape=[pltpu.VMEM(shape, queries.dtype) for shape in shapes],
+        in_specs=[pl.BlockSpec(memory_space=pltpu.SMEM), pl.BlockSpec(memory_space=pltpu.HBM)],
+        out_specs=[pl.BlockSpec(memory_space=pltpu.VMEM)] * 3,
+        scratch_shapes=[pltpu.SemaphoreType.DMA((3,))],
+        compiler_params=pltpu.CompilerParams(vmem_limit_bytes=8 * 2**20),
+        name="part",
+    )(row.astype(jnp.int32).reshape(1), queries)
 
 
 def paired(train_grads, query_grads):
@@ -51,7 +81,7 @@
     size, depth = queries.shape
     row, core = lax.axis_index("rows"), lax.axis_index("layers")
     z, x = row // 2, row % 2
-    ring = [(2 * a + b, 2 * ((a + 1) % count) + b) for a in range(count) for b in range(2)]
+    ring = [(2 * ((a + 1) % count) + b, 2 * a + b) for a in range(count) for b in range(2)]
     swap = [(a, a ^ 1) for a in range(rows)]
 
     def move(value, hops):
@@ -63,40 +93,50 @@
     def columns(value, which):
         return lax.dynamic_slice_in_dim(value, which * (depth // 2), depth // 2, 1)
 
-    cut = size // 2
-    low, high = queries[:, : depth // 2], queries[:, depth // 2 :]
-    held = jnp.where(x == 0, low, high)
-    given = [jnp.where(x == 0, high[rows], low[rows]) for rows in (slice(0, cut), slice(cut, size))]
-    firsts = {"A": held, "B": move(given[0], swap), "C": move(given[1], swap)}
+    cut = size * 9 // 16
+    rest = size - cut
+    held, given_b, given_c = parted(row, queries, cut)
+    firsts = {"A": held, "B": move(given_b, swap), "C": move(given_c, swap)}
     sides = {"O": columns(train, x), "N": move(columns(train, 1 - x), swap)}
+    heights = {"A": size, "B": cut, "C": rest}
+    starts = {"A": 0, "B": size, "C": size + cut}
+    held_at = [firsts]
+    for _ in range(1, count):
+        held_at.append({piece: move(value, ring) for piece, value in held_at[-1].items()})
+
+    def score(value, side):
+        return lax.optimization_barrier(product(value, sides[side]))
+
     partial = {}
-    for piece, value in firsts.items():
-        for step in range(count):
-            if step:
-                value = move(value, ring)
-            for side, rhs in sides.items():
-                partial[side, piece, step] = product(value, rhs)
+    for step, values in enumerate(held_at):
+        for side in sides:
+            if step < half:
+                whole = score(jnp.concatenate(list(values.values())), side)
+                for piece in values:
+                    first = starts[piece]
+                    partial[side, piece, step] = whole[first : first + heights[piece]]
+            else:
+                for piece, value in values.items():
+                    partial[side, piece, step] = score(value, side)
 
     total = None
     for group in range(half):
-        mine = lax.rem(z - group + count, count) // half == core
+        mine = lax.rem(z + group, count) // half == core
         sums, crossed = {}, {}
-        for pieces in ("A", "BC"):
+        for pieces in ("A", "BC") if group < half - 1 else "ABC":
             for side in "NO":
-                values = [partial[side, piece, step] for step in (group, group + half) for piece in pieces]
-                values = lax.optimization_barrier(values)
-                one, two = [jnp.concatenate(part) for part in (values[: len(pieces)], values[len(pieces) :])]
+                one, two = [
+                    jnp.concatenate([partial[side, piece, step] for piece in pieces]) for step in (group, group + half)
+                ]
                 keep, give = jnp.where(mine, one, two), jnp.where(mine, two, one)
                 sums[side] = [keep, cores(give)]
             got = move(sum(sums["N"]), swap)
             first = 0
             for piece in pieces:
-                height = size if piece == "A" else cut
-                for at in range(first, first + height, cut):
-                    key = (piece, at - first if piece == "A" else 0)
-                    crossed[key] = (got, at)
-                    sums[key] = [(value, at) for value in sums["O"]]
-                first += height
+                for low in (0, cut) if piece == "A" else (0,):
+                    crossed[piece, low] = (got, first + low)
+                    sums[piece, low] = [(value, first + low) for value in sums["O"]]
+                first += heights[piece]
         plan = []
         operands = []
 
@@ -107,14 +147,14 @@
             operands.append(value)
             return len(operands) - 1
 
-        for mine_key, their_key, across, at in (
-            (("A", 0), ("B", 0), False, 0),
-            (("A", cut), ("C", 0), False, cut),
-            (("B", 0), ("A", 0), True, 0),
-            (("C", 0), ("A", cut), True, cut),
+        for mine_key, their_key, across, at, span in (
+            (("A", 0), ("B", 0), False, 0, cut),
+            (("A", cut), ("C", 0), False, cut, rest),
+            (("B", 0), ("A", 0), True, 0, cut),
+            (("C", 0), ("A", cut), True, cut, rest),
         ):
             terms = [*sums[mine_key], crossed[their_key]]
-            plan.append((across, at, cut, [(index_of(value), first) for value, first in terms]))
+            plan.append((across, at, span, [(index_of(value), first) for value, first in terms]))
         specs = [pl.BlockSpec(memory_space=pltpu.SMEM)] + [pl.BlockSpec(memory_space=pltpu.VMEM)] * len(operands)
         aliases = {}
         if total is not None:

time: 166 us -> 156 us (0.940)
  starting transfers between devices: 21.9 us -> 43 us
  waiting for transfers between devices: 98.8 us -> 81.3 us
  matrix products: 35.4 us -> 21.3 us
  local copies, waits for them, and re-layouts: 3.36 us -> 6.89 us
  other arithmetic: 3.31 us -> 0.38 us
    ppermute x16 -> x17, starting transfers between devices: 20.3 us -> 40.4 us  [move(): return lax.ppermute(value, 'rows', hops)]
    ppermute x16 -> x17, waiting for transfers between devices: 98 us -> 79.3 us  [move(): return lax.ppermute(value, 'rows', hops)]
    dot_general x24 -> x16, matrix products: 35.4 us -> 21.3 us  [product(): return lax.dot_general(left, right, NT, preferred_element_type=jnp.float32)]
    select_n x2 -> x0, other arithmetic: 2.97 us -> none  [the longest x1 2.12 us: paired(): jnp.where(x == 0, high[rows], low[rows])]
    unnamed x14 -> x8, local copies, waits for them, and re-layouts: 1.96 us -> 4.63 us
  transfers between devices with their start and end apart: 24 -> 27, of which waited for: 13 -> 10; matrix products, arithmetic and copies ran while one was open for 24% -> 17% of each run, Pallas kernels for 1% -> 1%
where the time goes in v3:
time: 156 us
  waiting for transfers between devices  81.3 us (52%)
  starting transfers between devices  43 us (28%)
  matrix products  21.3 us (14%)
  local copies, waits for them, and re-layouts  6.89 us (4%)
  Pallas kernels  2.68 us (2%)
    ppermute x17, waiting for transfers between devices, move(): return lax.ppermute(value, 'rows', hops)  79.3 us
    ppermute x17, starting transfers between devices, move(): return lax.ppermute(value, 'rows', hops)  40.4 us
    dot_general x16, matrix products, product(): return lax.dot_general(left, right, NT, preferred_element_type=jnp.float32)  21.3 us
    unnamed x8, local copies, waits for them, and re-layouts  4.63 us
  transfers between devices with their start and end apart: 27, of which 10 were waited for; matrix products, arithmetic and copies ran while one was open for 17% of the time, Pallas kernels for 1%

profile of v3, /device:TPU:0, one launch (start us, length us, event | category | flops | bytes accessed | tf_op | source)
XLA Modules:
  0.0 155.9 jit_solution(16396604427029202937)
XLA Ops:
  0.0 1.4 copy-done.1
  1.4 1.0 part.1
  2.4 3.0 %collective-permute-start.1 = (bf16[72,2048]{1,0:T(8,128)(2,1)S(1)}, bf16[72,2048]{1,0:T(8,128)(2,1)}, u32[]{:S(2)}, u32[]{:S(2)}) collective-permute-start(bf16[72,2048]{1,0:T(8,128)(2,1)S(1)} %get-tuple-element.9), channel_id=1, source_target_pairs={{0,2},{2,0},{4,6},{6,4},{8,10},{10,8},{12,14},{14,12},{1,3},{3,1},... | collective-permute-start | bytes 884744 | tf_op jit(solution)/shard_map/ppermute | solution.py:88
  5.4 1.3 dynamic-slice_bitcast_fusion
  6.7 2.0 %collective-permute-start.3 = (bf16[56,2048]{1,0:T(8,128)(2,1)}, bf16[56,2048]{1,0:T(8,128)(2,1)}, u32[]{:S(2)}, u32[]{:S(2)}) collective-permute-start(bf16[56,2048]{1,0:T(8,128)(2,1)} %get-tuple-element.10), channel_id=1, source_target_pairs={{0,2},{2,0},{4,6},{6,4},{8,10},{10,8},{12,14},{14,12},{1,3},{3,1},... | collective-permute-start | bytes 688136 | tf_op jit(solution)/shard_map/ppermute | solution.py:88
  8.7 3.6 %collective-permute-start = (bf16[128,2048]{1,0:T(8,128)(2,1)}, bf16[128,2048]{1,0:T(8,128)(2,1)}, u32[]{:S(2)}, u32[]{:S(2)}) collective-permute-start(bf16[128,2048]{1,0:T(8,128)(2,1)} %get-tuple-element.8), channel_id=1, source_target_pairs={{4,0},{6,2},{8,4},{10,6},{12,8},{14,10},{0,12},{2,14},{5,1},{7,3},... | collective-permute-start | bytes 1572872 | tf_op jit(solution)/shard_map/ppermute | solution.py:88
  12.3 1.1 constant_dynamic-update-slice_fusion.5
  13.4 37.7 %collective-permute-done.3 = bf16[56,2048]{1,0:T(8,128)(2,1)} collective-permute-done((bf16[56,2048]{1,0:T(8,128)(2,1)}, bf16[56,2048]{1,0:T(8,128)(2,1)}, u32[]{:S(2)}, u32[]{:S(2)}) %collective-permute-start.3) | collective-permute-done | bytes 229408 | tf_op jit(solution)/shard_map/ppermute | solution.py:88
  51.1 3.8 %collective-permute-start.4 = (bf16[56,2048]{1,0:T(8,128)(2,1)}, bf16[56,2048]{1,0:T(8,128)(2,1)S(1)}, u32[]{:S(2)}, u32[]{:S(2)}) collective-permute-start(bf16[56,2048]{1,0:T(8,128)(2,1)} %collective-permute-done.3), channel_id=1, source_target_pairs={{4,0},{6,2},{8,4},{10,6},{12,8},{14,10},{0,12},{2,14},{5,1},{7,3},... | collective-permute-start | bytes 688136 | tf_op jit(solution)/shard_map/ppermute | solution.py:88
  55.5 1.0 constant_dynamic-update-slice_fusion.4
  56.5 1.0 constant_dynamic-update-slice_fusion.3
  57.4 0.7 fusion.6
  58.2 3.1 %collective-permute-done.4 = bf16[56,2048]{1,0:T(8,128)(2,1)S(1)} collective-permute-done((bf16[56,2048]{1,0:T(8,128)(2,1)}, bf16[56,2048]{1,0:T(8,128)(2,1)S(1)}, u32[]{:S(2)}, u32[]{:S(2)}) %collective-permute-start.4) | collective-permute-done | bytes 229408 | tf_op jit(solution)/shard_map/ppermute | solution.py:88
  61.3 4.2 %collective-permute-start.13 = (bf16[56,2048]{1,0:T(8,128)(2,1)S(1)}, bf16[56,2048]{1,0:T(8,128)(2,1)S(1)}, u32[]{:S(2)}, u32[]{:S(2)}) collective-permute-start(bf16[56,2048]{1,0:T(8,128)(2,1)S(1)} %collective-permute-done.4), channel_id=1, source_target_pairs={{4,0},{6,2},{8,4},{10,6},{12,8},{14,10},{0,12},{2,14},{5,1},{7,3},... | collective-permute-start | bytes 688136 | tf_op jit(solution)/shard_map/ppermute | solution.py:88
  65.5 1.1 constant_dynamic-update-slice_fusion.2
  66.6 1.0 collective-permute-done.2
  67.6 4.2 %collective-permute-start.9 = (bf16[72,2048]{1,0:T(8,128)(2,1)S(1)}, bf16[72,2048]{1,0:T(8,128)(2,1)S(1)}, u32[]{:S(2)}, u32[]{:S(2)}) collective-permute-start(bf16[72,2048]{1,0:T(8,128)(2,1)S(1)} %collective-permute-done.2), channel_id=1, source_target_pairs={{4,0},{6,2},{8,4},{10,6},{12,8},{14,10},{0,12},{2,14},{5,1},{7,3},... | collective-permute-start | bytes 884744 | tf_op jit(solution)/shard_map/ppermute | solution.py:88
  71.8 0.7 fusion.14
  72.6 0.6 fusion
  73.2 4.2 %collective-permute-start.14 = (bf16[56,2048]{1,0:T(8,128)(2,1)S(1)}, bf16[56,2048]{1,0:T(8,128)(2,1)S(1)}, u32[]{:S(2)}, u32[]{:S(2)}) collective-permute-start(bf16[56,2048]{1,0:T(8,128)(2,1)S(1)} %collective-permute-done.13), channel_id=1, source_target_pairs={{4,0},{6,2},{8,4},{10,6},{12,8},{14,10},{0,12},{2,14},{5,1},{7,3},... | collective-permute-start | bytes 688136 | tf_op jit(solution)/shard_map/ppermute | solution.py:88
  77.4 12.6 %collective-permute-done.9 = bf16[72,2048]{1,0:T(8,128)(2,1)S(1)} collective-permute-done((bf16[72,2048]{1,0:T(8,128)(2,1)S(1)}, bf16[72,2048]{1,0:T(8,128)(2,1)S(1)}, u32[]{:S(2)}, u32[]{:S(2)}) %collective-permute-start.9) | collective-permute-done | bytes 294944 | tf_op jit(solution)/shard_map/ppermute | solution.py:88
  90.0 0.6 fusion.2
  90.6 4.3 %collective-permute-start.10 = (bf16[72,2048]{1,0:T(8,128)(2,1)S(1)}, bf16[72,2048]{1,0:T(8,128)(2,1)S(1)}, u32[]{:S(2)}, u32[]{:S(2)}) collective-permute-start(bf16[72,2048]{1,0:T(8,128)(2,1)S(1)} %collective-permute-done.9), channel_id=1, source_target_pairs={{4,0},{6,2},{8,4},{10,6},{12,8},{14,10},{0,12},{2,14},{5,1},{7,3},... | collective-permute-start | bytes 884744 | tf_op jit(solution)/shard_map/ppermute | solution.py:88
  94.9 0.6 fusion.8
  95.6 0.6 fusion.4
  96.2 4.1 %collective-permute-start.6 = (bf16[128,2048]{1,0:T(8,128)(2,1)S(1)}, bf16[128,2048]{1,0:T(8,128)(2,1)S(1)}, u32[]{:S(2)}, u32[]{:S(2)}) collective-permute-start(bf16[128,2048]{1,0:T(8,128)(2,1)S(1)} %collective-permute-done.5), channel_id=1, source_target_pairs={{4,0},{6,2},{8,4},{10,6},{12,8},{14,10},{0,12},{2,14},{5,1},{7,3},... | collective-permute-start | bytes 1572872 | tf_op jit(solution)/shard_map/ppermute | solution.py:88
  100.9 0.6 fusion.10
  101.6 10.6 %collective-permute-done.6 = bf16[128,2048]{1,0:T(8,128)(2,1)S(1)} collective-permute-done((bf16[128,2048]{1,0:T(8,128)(2,1)S(1)}, bf16[128,2048]{1,0:T(8,128)(2,1)S(1)}, u32[]{:S(2)}, u32[]{:S(2)}) %collective-permute-start.6) | collective-permute-done | bytes 524320 | tf_op jit(solution)/shard_map/ppermute | solution.py:88
  112.1 0.6 fusion.12
  112.8 2.1 %fusion.36 = f32[256,384]{1,0:T(8,128)S(1)} fusion(bf16[256,2048]{1,0:T(8,128)(2,1)S(1)} %constant_dynamic-update-slice_fusion.3, bf16[384,2048]{1,0:T(8,128)(2,1)} %collective-permute-done.8), kind=kOutput, calls=%fused_computation.65 | convolution fusion | flops 402653184 | bytes 3014656 | tf_op jit(solution)/shard_map/dot_general | solution.py:16
  114.9 2.0 %fusion.39 = f32[128,384]{1,0:T(8,128)S(1)} fusion(bf16[128,2048]{1,0:T(8,128)(2,1)S(1)} %collective-permute-done.5, bf16[384,2048]{1,0:T(8,128)(2,1)} %collective-permute-done.8), kind=kOutput, calls=%fused_computation.68 | convolution fusion | flops 201326592 | bytes 2293760 | tf_op jit(solution)/shard_map/dot_general | solution.py:16
  117.1 2.1 %fusion.32 = f32[256,384]{1,0:T(8,128)S(1)} fusion(bf16[256,2048]{1,0:T(8,128)(2,1)S(1)} %constant_dynamic-update-slice_fusion, bf16[384,2048]{1,0:T(8,128)(2,1)} %collective-permute-done.8), kind=kOutput, calls=%fused_computation.61 | convolution fusion | flops 402653184 | bytes 3014656 | tf_op jit(solution)/shard_map/dot_general | solution.py:16
  119.2 2.0 %fusion.35 = f32[128,384]{1,0:T(8,128)S(1)} fusion(bf16[128,2048]{1,0:T(8,128)(2,1)S(1)} %collective-permute-done.6, bf16[384,2048]{1,0:T(8,128)(2,1)} %collective-permute-done.8), kind=kOutput, calls=%fused_computation.64 | convolution fusion | flops 201326592 | bytes 2293760 | tf_op jit(solution)/shard_map/dot_general | solution.py:16
  121.2 2.0 %fusion.34 = f32[56,384]{1,0:T(8,128)S(1)} fusion(bf16[56,2048]{1,0:T(8,128)(2,1)S(1)} %collective-permute-done.14, bf16[384,2048]{1,0:T(8,128)(2,1)} %collective-permute-done.8), kind=kOutput, calls=%fused_computation.63 | convolution fusion | flops 88080384 | bytes 1888256 | tf_op jit(solution)/shard_map/dot_general | solution.py:16
  123.2 2.0 %fusion.33 = f32[72,384]{1,0:T(8,128)S(1)} fusion(bf16[72,2048]{1,0:T(8,128)(2,1)S(1)} %collective-permute-done.10, bf16[384,2048]{1,0:T(8,128)(2,1)} %collective-permute-done.8), kind=kOutput, calls=%fused_computation.62 | convolution fusion | flops 113246208 | bytes 1978368 | tf_op jit(solution)/shard_map/dot_general | solution.py:16
  125.8 2.0 %fusion.37 = f32[72,384]{1,0:T(8,128)S(1)} fusion(bf16[72,2048]{1,0:T(8,128)(2,1)S(1)} %collective-permute-done.9, bf16[384,2048]{1,0:T(8,128)(2,1)} %collective-permute-done.8), kind=kOutput, calls=%fused_computation.66 | convolution fusion | flops 113246208 | bytes 1978368 | tf_op jit(solution)/shard_map/dot_general | solution.py:16
  127.8 2.0 %fusion.38 = f32[56,384]{1,0:T(8,128)S(1)} fusion(bf16[56,2048]{1,0:T(8,128)(2,1)S(1)} %collective-permute-done.13, bf16[384,2048]{1,0:T(8,128)(2,1)} %collective-permute-done.8), kind=kOutput, calls=%fused_computation.67 | convolution fusion | flops 88080384 | bytes 1888256 | tf_op jit(solution)/shard_map/dot_general | solution.py:16
  130.6 0.8 collective-permute-done.18
  131.5 1.3 collective-permute-done.22
  132.8 1.5 collective-permute-start.26
  135.5 1.5 collective-permute-start.19
  137.0 3.6 %collective-permute-done.26.refs_5_ = f32[128,384]{1,0:T(8,128)S(1)} collective-permute-done((f32[128,384]{1,0:T(8,128)S(1)}, f32[128,384]{1,0:T(8,128)S(1)}, u32[]{:S(2)}, u32[]{:S(2)}) %collective-permute-start.26) | collective-permute-done | bytes 196640 | tf_op jit(solution)/shard_map/ppermute | solution.py:88
  140.6 1.5 collective-permute-start.23
  142.1 8.5 %collective-permute-done.23.refs_2_ = f32[128,384]{1,0:T(8,128)S(1)} collective-permute-done((f32[128,384]{1,0:T(8,128)S(1)}, f32[128,384]{1,0:T(8,128)S(1)}, u32[]{:S(2)}, u32[]{:S(2)}) %collective-permute-start.23) | collective-permute-done | bytes 196640 | tf_op jit(solution)/shard_map/ppermute | solution.py:88
  150.5 1.5 collective-permute-start.16
  152.0 0.9 shard_map.28.refs_9_
  152.9 2.1 %collective-permute-done.16.refs_3_ = f32[56,384]{1,0:T(8,128)S(1)} collective-permute-done((f32[56,384]{1,0:T(8,128)S(1)}, f32[56,384]{1,0:T(8,128)S(1)}, u32[]{:S(2)}, u32[]{:S(2)}) %collective-permute-start.16) | collective-permute-done | bytes 86048 | tf_op jit(solution)/shard_map/ppermute | solution.py:88
  155.0 0.8 shard_map.29
  (49 shorter events, 4.1 us)
Async XLA Ops:
  0.0 5.4 %copy-start = (bf16[384,1,4096]{2,0,1:T(8,128)(2,1)S(1)}, bf16[384,1,4096]{2,0,1:T(8,128)(2,1)}, u32[]{:S(2)}) copy-start(bf16[384,1,4096]{2,0,1:T(8,128)(2,1)} %param.2) | copy-start | bytes 9437188
  0.0 1.4 copy-start.1
  2.4 52.6 %collective-permute-start.1 = (bf16[72,2048]{1,0:T(8,128)(2,1)S(1)}, bf16[72,2048]{1,0:T(8,128)(2,1)}, u32[]{:S(2)}, u32[]{:S(2)}) collective-permute-start(bf16[72,2048]{1,0:T(8,128)(2,1)S(1)} %get-tuple-element.9), channel_id=1, source_target_pairs={{0,2},{2,0},{4,6},{6,4},{8,10},{10,8},{12,14},{14,12},{1,3},{3,1},... | collective-permute-start | bytes 884744 | tf_op jit(solution)/shard_map/ppermute | solution.py:88
  6.7 106.1 %collective-permute-start.8 = (bf16[384,2048]{1,0:T(8,128)(2,1)}, bf16[384,2048]{1,0:T(8,128)(2,1)}, u32[]{:S(2)}, u32[]{:S(2)}) collective-permute-start(bf16[384,2048]{1,0:T(8,128)(2,1)} %dynamic-slice_bitcast_fusion), channel_id=1, source_target_pairs={{0,2},{2,0},{4,6},{6,4},{8,10},{10,8},{12,14},{14,12},{1,3},{3,1},... | collective-permute-start | bytes 4718600 | tf_op jit(solution)/shard_map/ppermute | solution.py:88
  6.7 44.4 %collective-permute-start.3 = (bf16[56,2048]{1,0:T(8,128)(2,1)}, bf16[56,2048]{1,0:T(8,128)(2,1)}, u32[]{:S(2)}, u32[]{:S(2)}) collective-permute-start(bf16[56,2048]{1,0:T(8,128)(2,1)} %get-tuple-element.10), channel_id=1, source_target_pairs={{0,2},{2,0},{4,6},{6,4},{8,10},{10,8},{12,14},{14,12},{1,3},{3,1},... | collective-permute-start | bytes 688136 | tf_op jit(solution)/shard_map/ppermute | solution.py:88
  8.7 56.8 %collective-permute-start = (bf16[128,2048]{1,0:T(8,128)(2,1)}, bf16[128,2048]{1,0:T(8,128)(2,1)}, u32[]{:S(2)}, u32[]{:S(2)}) collective-permute-start(bf16[128,2048]{1,0:T(8,128)(2,1)} %get-tuple-element.8), channel_id=1, source_target_pairs={{4,0},{6,2},{8,4},{10,6},{12,8},{14,10},{0,12},{2,14},{5,1},{7,3},... | collective-permute-start | bytes 1572872 | tf_op jit(solution)/shard_map/ppermute | solution.py:88
  51.1 10.2 %collective-permute-start.4 = (bf16[56,2048]{1,0:T(8,128)(2,1)}, bf16[56,2048]{1,0:T(8,128)(2,1)S(1)}, u32[]{:S(2)}, u32[]{:S(2)}) collective-permute-start(bf16[56,2048]{1,0:T(8,128)(2,1)} %collective-permute-done.3), channel_id=1, source_target_pairs={{4,0},{6,2},{8,4},{10,6},{12,8},{14,10},{0,12},{2,14},{5,1},{7,3},... | collective-permute-start | bytes 688136 | tf_op jit(solution)/shard_map/ppermute | solution.py:88
  55.0 12.6 %collective-permute-start.2 = (bf16[72,2048]{1,0:T(8,128)(2,1)}, bf16[72,2048]{1,0:T(8,128)(2,1)S(1)}, u32[]{:S(2)}, u32[]{:S(2)}) collective-permute-start(bf16[72,2048]{1,0:T(8,128)(2,1)} %collective-permute-done.1), channel_id=1, source_target_pairs={{4,0},{6,2},{8,4},{10,6},{12,8},{14,10},{0,12},{2,14},{5,1},{7,3},... | collective-permute-start | bytes 884744 | tf_op jit(solution)/shard_map/ppermute | solution.py:88
  61.3 11.3 %collective-permute-start.13 = (bf16[56,2048]{1,0:T(8,128)(2,1)S(1)}, bf16[56,2048]{1,0:T(8,128)(2,1)S(1)}, u32[]{:S(2)}, u32[]{:S(2)}) collective-permute-start(bf16[56,2048]{1,0:T(8,128)(2,1)S(1)} %collective-permute-done.4), channel_id=1, source_target_pairs={{4,0},{6,2},{8,4},{10,6},{12,8},{14,10},{0,12},{2,14},{5,1},{7,3},... | collective-permute-start | bytes 688136 | tf_op jit(solution)/shard_map/ppermute | solution.py:88
  65.5 30.1 %collective-permute-start.5 = (bf16[128,2048]{1,0:T(8,128)(2,1)}, bf16[128,2048]{1,0:T(8,128)(2,1)S(1)}, u32[]{:S(2)}, u32[]{:S(2)}) collective-permute-start(bf16[128,2048]{1,0:T(8,128)(2,1)} %collective-permute-done), channel_id=1, source_target_pairs={{4,0},{6,2},{8,4},{10,6},{12,8},{14,10},{0,12},{2,14},{5,1},{7,3},... | collective-permute-start | bytes 1572872 | tf_op jit(solution)/shard_map/ppermute | solution.py:88
  67.6 22.4 %collective-permute-start.9 = (bf16[72,2048]{1,0:T(8,128)(2,1)S(1)}, bf16[72,2048]{1,0:T(8,128)(2,1)S(1)}, u32[]{:S(2)}, u32[]{:S(2)}) collective-permute-start(bf16[72,2048]{1,0:T(8,128)(2,1)S(1)} %collective-permute-done.2), channel_id=1, source_target_pairs={{4,0},{6,2},{8,4},{10,6},{12,8},{14,10},{0,12},{2,14},{5,1},{7,3},... | collective-permute-start | bytes 884744 | tf_op jit(solution)/shard_map/ppermute | solution.py:88
  73.2 21.7 %collective-permute-start.14 = (bf16[56,2048]{1,0:T(8,128)(2,1)S(1)}, bf16[56,2048]{1,0:T(8,128)(2,1)S(1)}, u32[]{:S(2)}, u32[]{:S(2)}) collective-permute-start(bf16[56,2048]{1,0:T(8,128)(2,1)S(1)} %collective-permute-done.13), channel_id=1, source_target_pairs={{4,0},{6,2},{8,4},{10,6},{12,8},{14,10},{0,12},{2,14},{5,1},{7,3},... | collective-permute-start | bytes 688136 | tf_op jit(solution)/shard_map/ppermute | solution.py:88
  90.6 10.0 %collective-permute-start.10 = (bf16[72,2048]{1,0:T(8,128)(2,1)S(1)}, bf16[72,2048]{1,0:T(8,128)(2,1)S(1)}, u32[]{:S(2)}, u32[]{:S(2)}) collective-permute-start(bf16[72,2048]{1,0:T(8,128)(2,1)S(1)} %collective-permute-done.9), channel_id=1, source_target_pairs={{4,0},{6,2},{8,4},{10,6},{12,8},{14,10},{0,12},{2,14},{5,1},{7,3},... | collective-permute-start | bytes 884744 | tf_op jit(solution)/shard_map/ppermute | solution.py:88
  95.5 38.8 %collective-permute-start.20 = (f32[56,384]{1,0:T(8,128)S(1)}, f32[56,384]{1,0:T(8,128)S(1)}, u32[]{:S(2)}, u32[]{:S(2)}) collective-permute-start(f32[56,384]{1,0:T(8,128)S(1)} %get-tuple-element.19), channel_id=1, source_target_pairs={{0,1},{1,0},{2,3},{3,2},{4,5},{5,4},{6,7},{7,6},{8,9},{9,8},{10,11... | collective-permute-start | bytes 258056 | tf_op jit(solution)/shard_map/ppermute | solution.py:91
  96.2 15.9 %collective-permute-start.6 = (bf16[128,2048]{1,0:T(8,128)(2,1)S(1)}, bf16[128,2048]{1,0:T(8,128)(2,1)S(1)}, u32[]{:S(2)}, u32[]{:S(2)}) collective-permute-start(bf16[128,2048]{1,0:T(8,128)(2,1)S(1)} %collective-permute-done.5), channel_id=1, source_target_pairs={{4,0},{6,2},{8,4},{10,6},{12,8},{14,10},{0,12},{2,14},{5,1},{7,3},... | collective-permute-start | bytes 1572872 | tf_op jit(solution)/shard_map/ppermute | solution.py:88
  100.4 34.1 %collective-permute-start.21 = (f32[128,384]{1,0:T(8,128)S(1)}, f32[128,384]{1,0:T(8,128)S(1)}, u32[]{:S(2)}, u32[]{:S(2)}) collective-permute-start(f32[128,384]{1,0:T(8,128)S(1)} %get-tuple-element.24), channel_id=1, source_target_pairs={{0,1},{1,0},{2,3},{3,2},{4,5},{5,4},{6,7},{7,6},{8,9},{9,8},{10,11... | collective-permute-start | bytes 589832 | tf_op jit(solution)/shard_map/ppermute | solution.py:91
  100.6 34.3 %collective-permute-start.24 = (f32[128,384]{1,0:T(8,128)S(1)}, f32[128,384]{1,0:T(8,128)S(1)}, u32[]{:S(2)}, u32[]{:S(2)}) collective-permute-start(f32[128,384]{1,0:T(8,128)S(1)} %get-tuple-element.11), channel_id=1, source_target_pairs={{0,1},{1,0},{2,3},{3,2},{4,5},{5,4},{6,7},{7,6},{8,9},{9,8},{10,11... | collective-permute-start | bytes 589832 | tf_op jit(solution)/shard_map/ppermute | solution.py:91
  117.0 13.0 %collective-permute-start.25 = (f32[128,384]{1,0:T(8,128)S(1)}, f32[128,384]{1,0:T(8,128)S(1)}, u32[]{:S(2)}, u32[]{:S(2)}) collective-permute-start(f32[128,384]{1,0:T(8,128)S(1)} %slice_select_fusion), channel_id=1, source_target_pairs={{0,1},{1,0},{2,3},{3,2},{4,5},{5,4},{6,7},{7,6},{8,9},{9,8},{10,11... | collective-permute-start | bytes 589832 | tf_op jit(solution)/shard_map/ppermute | solution.py:91
  125.3 4.6 %collective-permute-start.11 = (f32[72,384]{1,0:T(8,128)S(1)}, f32[72,384]{1,0:T(8,128)S(1)}, u32[]{:S(2)}, u32[]{:S(2)}) collective-permute-start(f32[72,384]{1,0:T(8,128)S(1)} %slice_select_fusion.11), channel_id=1, source_target_pairs={{0,1},{1,0},{2,3},{3,2},{4,5},{5,4},{6,7},{7,6},{8,9},{9,8},{10,11... | collective-permute-start | bytes 331784 | tf_op jit(solution)/shard_map/ppermute | solution.py:91
  129.9 1.5 collective-permute-start.18
  130.0 5.5 %collective-permute-start.15 = (f32[56,384]{1,0:T(8,128)S(1)}, f32[56,384]{1,0:T(8,128)S(1)}, u32[]{:S(2)}, u32[]{:S(2)}) collective-permute-start(f32[56,384]{1,0:T(8,128)S(1)} %slice_select_fusion.14), channel_id=1, source_target_pairs={{0,1},{1,0},{2,3},{3,2},{4,5},{5,4},{6,7},{7,6},{8,9},{9,8},{10,11... | collective-permute-start | bytes 258056 | tf_op jit(solution)/shard_map/ppermute | solution.py:91
  131.4 1.4 collective-permute-start.22
  132.8 7.8 %collective-permute-start.26 = (f32[128,384]{1,0:T(8,128)S(1)}, f32[128,384]{1,0:T(8,128)S(1)}, u32[]{:S(2)}, u32[]{:S(2)}) collective-permute-start(f32[128,384]{1,0:T(8,128)S(1)} %get-tuple-element.21), channel_id=1, source_target_pairs={{0,2},{2,0},{4,6},{6,4},{8,10},{10,8},{12,14},{14,12},{1,3},{3,1},... | collective-permute-start | bytes 589832 | tf_op jit(solution)/shard_map/ppermute | solution.py:88
  134.3 18.6 %collective-permute-start.17 = (f32[72,384]{1,0:T(8,128)S(1)}, f32[72,384]{1,0:T(8,128)S(1)}, u32[]{:S(2)}, u32[]{:S(2)}) collective-permute-start(f32[72,384]{1,0:T(8,128)S(1)} %get-tuple-element.17), channel_id=1, source_target_pairs={{0,1},{1,0},{2,3},{3,2},{4,5},{5,4},{6,7},{7,6},{8,9},{9,8},{10,11... | collective-permute-start | bytes 331784 | tf_op jit(solution)/shard_map/ppermute | solution.py:91
  134.4 20.6 %collective-permute-start.7 = (f32[128,384]{1,0:T(8,128)S(1)}, f32[128,384]{1,0:T(8,128)S(1)}, u32[]{:S(2)}, u32[]{:S(2)}) collective-permute-start(f32[128,384]{1,0:T(8,128)S(1)} %get-tuple-element.15), channel_id=1, source_target_pairs={{0,1},{1,0},{2,3},{3,2},{4,5},{5,4},{6,7},{7,6},{8,9},{9,8},{10,11... | collective-permute-start | bytes 589832 | tf_op jit(solution)/shard_map/ppermute | solution.py:91
  134.9 20.1 %collective-permute-start.12 = (f32[72,384]{1,0:T(8,128)S(1)}, f32[72,384]{1,0:T(8,128)S(1)}, u32[]{:S(2)}, u32[]{:S(2)}) collective-permute-start(f32[72,384]{1,0:T(8,128)S(1)} %select_add_fusion.3), channel_id=1, source_target_pairs={{0,2},{2,0},{4,6},{6,4},{8,10},{10,8},{12,14},{14,12},{1,3},{3,1},... | collective-permute-start | bytes 331784 | tf_op jit(solution)/shard_map/ppermute | solution.py:88
  135.5 19.6 %collective-permute-start.19 = (f32[128,384]{1,0:T(8,128)S(1)}, f32[128,384]{1,0:T(8,128)S(1)}, u32[]{:S(2)}, u32[]{:S(2)}) collective-permute-start(f32[128,384]{1,0:T(8,128)S(1)} %select_add_fusion.2), channel_id=1, source_target_pairs={{0,2},{2,0},{4,6},{6,4},{8,10},{10,8},{12,14},{14,12},{1,3},{3,1},... | collective-permute-start | bytes 589832 | tf_op jit(solution)/shard_map/ppermute | solution.py:88
  140.6 10.0 %collective-permute-start.23 = (f32[128,384]{1,0:T(8,128)S(1)}, f32[128,384]{1,0:T(8,128)S(1)}, u32[]{:S(2)}, u32[]{:S(2)}) collective-permute-start(f32[128,384]{1,0:T(8,128)S(1)} %select_add_fusion.1), channel_id=1, source_target_pairs={{0,2},{2,0},{4,6},{6,4},{8,10},{10,8},{12,14},{14,12},{1,3},{3,1},... | collective-permute-start | bytes 589832 | tf_op jit(solution)/shard_map/ppermute | solution.py:88
  150.5 4.5 %collective-permute-start.16 = (f32[56,384]{1,0:T(8,128)S(1)}, f32[56,384]{1,0:T(8,128)S(1)}, u32[]{:S(2)}, u32[]{:S(2)}) collective-permute-start(f32[56,384]{1,0:T(8,128)S(1)} %select_add_fusion.4), channel_id=1, source_target_pairs={{0,2},{2,0},{4,6},{6,4},{8,10},{10,8},{12,14},{14,12},{1,3},{3,1},... | collective-permute-start | bytes 258056 | tf_op jit(solution)/shard_map/ppermute | solution.py:88

commit v4 on v3

--- a/solution.py
+++ b/solution.py
@@ -43,33 +43,32 @@
     copy.wait()
 
 
-def part(cut, row_ref, queries_ref, held_ref, b_ref, c_ref, sems):
+def part(spans, row_ref, whole_ref, *refs):
+    held_ref, given_refs, sems = refs[0], refs[1:-1], refs[-1]
     half = held_ref.shape[1]
     x = row_ref[0] % 2
     mine, other = (pl.ds(pl.multiple_of(side * half, half), half) for side in (x, 1 - x))
-    copies = [
-        pltpu.make_async_copy(queries_ref.at[:, mine], held_ref, sems.at[0]),
-        pltpu.make_async_copy(queries_ref.at[:cut, other], b_ref, sems.at[1]),
-        pltpu.make_async_copy(queries_ref.at[cut:, other], c_ref, sems.at[2]),
-    ]
+    copies = [pltpu.make_async_copy(whole_ref.at[:, mine], held_ref, sems.at[0])]
+    for i, (first, end) in enumerate(spans):
+        copies.append(pltpu.make_async_copy(whole_ref.at[first:end, other], given_refs[i], sems.at[i + 1]))
     for copy in copies:
         copy.start()
     for copy in copies:
         copy.wait()
 
 
-def parted(row, queries, cut):
-    size, depth = queries.shape
-    shapes = [(size, depth // 2), (cut, depth // 2), (size - cut, depth // 2)]
+def parted(row, whole, cuts):
+    size, depth = whole.shape
+    spans = list(zip((0, *cuts), (*cuts, size)))
+    shapes = [(size, depth // 2)] + [(end - first, depth // 2) for first, end in spans]
     return pl.pallas_call(
-        functools.partial(part, cut),
-        out_shape=[pltpu.VMEM(shape, queries.dtype) for shape in shapes],
+        functools.partial(part, spans),
+        out_shape=[pltpu.VMEM(shape, whole.dtype) for shape in shapes],
         in_specs=[pl.BlockSpec(memory_space=pltpu.SMEM), pl.BlockSpec(memory_space=pltpu.HBM)],
-        out_specs=[pl.BlockSpec(memory_space=pltpu.VMEM)] * 3,
-        scratch_shapes=[pltpu.SemaphoreType.DMA((3,))],
+        out_specs=[pl.BlockSpec(memory_space=pltpu.VMEM)] * len(shapes),
+        scratch_shapes=[pltpu.SemaphoreType.DMA((len(shapes),))],
         compiler_params=pltpu.CompilerParams(vmem_limit_bytes=8 * 2**20),
-        name="part",
-    )(row.astype(jnp.int32).reshape(1), queries)
+    )(row.astype(jnp.int32).reshape(1), pltpu.with_memory_space_constraint(whole, pltpu.HBM))
 
 
 def paired(train_grads, query_grads):
@@ -78,9 +77,9 @@
     half = count // layers
     train = train_grads.reshape(train_grads.shape[0], -1)
     queries = jnp.swapaxes(query_grads, 0, 1).reshape(query_grads.shape[1], -1)
-    size, depth = queries.shape
+    size, _ = queries.shape
     row, core = lax.axis_index("rows"), lax.axis_index("layers")
-    z, x = row // 2, row % 2
+    z = row // 2
     ring = [(2 * ((a + 1) % count) + b, 2 * a + b) for a in range(count) for b in range(2)]
     swap = [(a, a ^ 1) for a in range(rows)]
 
@@ -90,14 +89,12 @@
     def cores(value):
         return lax.ppermute(value, "layers", [(0, 1), (1, 0)])
 
-    def columns(value, which):
-        return lax.dynamic_slice_in_dim(value, which * (depth // 2), depth // 2, 1)
-
     cut = size * 9 // 16
     rest = size - cut
-    held, given_b, given_c = parted(row, queries, cut)
+    held, given_b, given_c = parted(row, queries, (cut,))
     firsts = {"A": held, "B": move(given_b, swap), "C": move(given_c, swap)}
-    sides = {"O": columns(train, x), "N": move(columns(train, 1 - x), swap)}
+    train_held, train_given = parted(row, train, ())
+    sides = {"O": train_held, "N": move(train_given, swap)}
     heights = {"A": size, "B": cut, "C": rest}
     starts = {"A": 0, "B": size, "C": size + cut}
     held_at = [firsts]

time: 156 us -> 125 us (0.80)
  waiting for transfers between devices: 81.3 us -> 55.3 us
  local copies, waits for them, and re-layouts: 6.89 us -> 1.09 us
  Pallas kernels: 2.68 us -> 5.98 us
  starting transfers between devices: 43 us -> 40.6 us
    ppermute x17, waiting for transfers between devices: 79.3 us -> 53.2 us  [move(): return lax.ppermute(value, 'rows', hops)]
    unnamed x8 -> x4, local copies, waits for them, and re-layouts: 4.63 us -> 0.12 us
    pallas_call x1 -> x2, Pallas kernels: 0.99 us -> 4.29 us  [parted(): pl.pallas_call(functools.partial(part, spans), out_shape=[pltpu.VMEM(shap...]
    ppermute x17, starting transfers between devices: 40.4 us -> 38 us  [move(): return lax.ppermute(value, 'rows', hops)]
  transfers between devices with their start and end apart: 27 -> 27, of which waited for: 10 -> 10; matrix products, arithmetic and copies ran while one was open for 17% -> 18% of each run, Pallas kernels for 1% -> 3%
where the time goes in v4:
time: 125 us
  waiting for transfers between devices  55.3 us (44%)
  starting transfers between devices  40.6 us (32%)
  matrix products  21.2 us (17%)
  Pallas kernels  5.98 us (5%)
    ppermute x17, waiting for transfers between devices, move(): return lax.ppermute(value, 'rows', hops)  53.2 us
    ppermute x17, starting transfers between devices, move(): return lax.ppermute(value, 'rows', hops)  38 us
    dot_general x16, matrix products, product(): return lax.dot_general(left, right, NT, preferred_element_type=jnp.float32)  21.2 us
    pallas_call x2, Pallas kernels, parted(): pl.pallas_call(functools.partial(part, spans), out_shape=[pltpu.VMEM(shap...  4.29 us
    ppermute x10, starting transfers between devices, cores(): return lax.ppermute(value, 'layers', [(0, 1), (1, 0)])  2.61 us
  transfers between devices with their start and end apart: 27, of which 10 were waited for; matrix products, arithmetic and copies ran while one was open for 18% of the time, Pallas kernels for 3%

profile of v4, /device:TPU:0, one launch (start us, length us, event | category | flops | bytes accessed | tf_op | source)
XLA Modules:
  0.0 124.9 jit_solution(10726005842536401422)
XLA Ops:
  0.0 1.2 shard_map.28
  1.2 3.0 %collective-permute-start.1 = (bf16[72,2048]{1,0:T(8,128)(2,1)S(1)}, bf16[72,2048]{1,0:T(8,128)(2,1)S(1)}, u32[]{:S(2)}, u32[]{:S(2)}) collective-permute-start(bf16[72,2048]{1,0:T(8,128)(2,1)S(1)} %get-tuple-element.11), channel_id=1, source_target_pairs={{0,2},{2,0},{4,6},{6,4},{8,10},{10,8},{12,14},{14,12},{1,3},{3,1},... | collective-permute-start | bytes 884744 | tf_op jit(solution)/shard_map/ppermute | solution.py:87
  4.3 3.1 %shard_map.29 = (bf16[384,2048]{1,0:T(8,128)(2,1)S(1)}, bf16[384,2048]{1,0:T(8,128)(2,1)}) custom-call(s32[1]{0:T(128)} %bitcast.row_ref, bf16[384,4096]{1,0:T(8,128)(2,1)} %bitcast.35), custom_call_target="tpu_custom_call" | custom-call | tf_op jit(solution)/shard_map/pallas_call | solution.py:64
  7.4 2.0 %collective-permute-start.8 = (bf16[384,2048]{1,0:T(8,128)(2,1)}, bf16[384,2048]{1,0:T(8,128)(2,1)}, u32[]{:S(2)}, u32[]{:S(2)}) collective-permute-start(bf16[384,2048]{1,0:T(8,128)(2,1)} %get-tuple-element.14), channel_id=1, source_target_pairs={{0,2},{2,0},{4,6},{6,4},{8,10},{10,8},{12,14},{14,12},{1,3},{3,1},... | collective-permute-start | bytes 4718600 | tf_op jit(solution)/shard_map/ppermute | solution.py:87
  9.4 3.6 %collective-permute-start = (bf16[128,2048]{1,0:T(8,128)(2,1)S(1)}, bf16[128,2048]{1,0:T(8,128)(2,1)S(1)}, u32[]{:S(2)}, u32[]{:S(2)}) collective-permute-start(bf16[128,2048]{1,0:T(8,128)(2,1)S(1)} %get-tuple-element.10), channel_id=1, source_target_pairs={{4,0},{6,2},{8,4},{10,6},{12,8},{14,10},{0,12},{2,14},{5,1},{7,3},... | collective-permute-start | bytes 1572872 | tf_op jit(solution)/shard_map/ppermute | solution.py:87
  13.1 4.0 %collective-permute-done.3 = bf16[56,2048]{1,0:T(8,128)(2,1)} collective-permute-done((bf16[56,2048]{1,0:T(8,128)(2,1)S(1)}, bf16[56,2048]{1,0:T(8,128)(2,1)}, u32[]{:S(2)}, u32[]{:S(2)}) %collective-permute-start.3) | collective-permute-done | bytes 229408 | tf_op jit(solution)/shard_map/ppermute | solution.py:87
  17.1 4.1 %collective-permute-start.4 = (bf16[56,2048]{1,0:T(8,128)(2,1)}, bf16[56,2048]{1,0:T(8,128)(2,1)S(1)}, u32[]{:S(2)}, u32[]{:S(2)}) collective-permute-start(bf16[56,2048]{1,0:T(8,128)(2,1)} %collective-permute-done.3), channel_id=1, source_target_pairs={{4,0},{6,2},{8,4},{10,6},{12,8},{14,10},{0,12},{2,14},{5,1},{7,3},... | collective-permute-start | bytes 688136 | tf_op jit(solution)/shard_map/ppermute | solution.py:87
  21.7 1.0 constant_dynamic-update-slice_fusion.3
  22.7 0.7 fusion.8
  23.4 6.9 %collective-permute-done.4 = bf16[56,2048]{1,0:T(8,128)(2,1)S(1)} collective-permute-done((bf16[56,2048]{1,0:T(8,128)(2,1)}, bf16[56,2048]{1,0:T(8,128)(2,1)S(1)}, u32[]{:S(2)}, u32[]{:S(2)}) %collective-permute-start.4) | collective-permute-done | bytes 229408 | tf_op jit(solution)/shard_map/ppermute | solution.py:87
  30.4 4.2 %collective-permute-start.13 = (bf16[56,2048]{1,0:T(8,128)(2,1)S(1)}, bf16[56,2048]{1,0:T(8,128)(2,1)S(1)}, u32[]{:S(2)}, u32[]{:S(2)}) collective-permute-start(bf16[56,2048]{1,0:T(8,128)(2,1)S(1)} %collective-permute-done.4), channel_id=1, source_target_pairs={{4,0},{6,2},{8,4},{10,6},{12,8},{14,10},{0,12},{2,14},{5,1},{7,3},... | collective-permute-start | bytes 688136 | tf_op jit(solution)/shard_map/ppermute | solution.py:87
  34.6 2.0 %collective-permute-done.2 = bf16[72,2048]{1,0:T(8,128)(2,1)S(1)} collective-permute-done((bf16[72,2048]{1,0:T(8,128)(2,1)S(1)}, bf16[72,2048]{1,0:T(8,128)(2,1)S(1)}, u32[]{:S(2)}, u32[]{:S(2)}) %collective-permute-start.2) | collective-permute-done | bytes 294944 | tf_op jit(solution)/shard_map/ppermute | solution.py:87
  36.6 4.3 %collective-permute-start.9 = (bf16[72,2048]{1,0:T(8,128)(2,1)S(1)}, bf16[72,2048]{1,0:T(8,128)(2,1)S(1)}, u32[]{:S(2)}, u32[]{:S(2)}) collective-permute-start(bf16[72,2048]{1,0:T(8,128)(2,1)S(1)} %collective-permute-done.2), channel_id=1, source_target_pairs={{4,0},{6,2},{8,4},{10,6},{12,8},{14,10},{0,12},{2,14},{5,1},{7,3},... | collective-permute-start | bytes 884744 | tf_op jit(solution)/shard_map/ppermute | solution.py:87
  40.9 0.7 fusion
  41.7 0.6 fusion.14
  42.2 4.2 %collective-permute-start.14 = (bf16[56,2048]{1,0:T(8,128)(2,1)S(1)}, bf16[56,2048]{1,0:T(8,128)(2,1)S(1)}, u32[]{:S(2)}, u32[]{:S(2)}) collective-permute-start(bf16[56,2048]{1,0:T(8,128)(2,1)S(1)} %collective-permute-done.13), channel_id=1, source_target_pairs={{4,0},{6,2},{8,4},{10,6},{12,8},{14,10},{0,12},{2,14},{5,1},{7,3},... | collective-permute-start | bytes 688136 | tf_op jit(solution)/shard_map/ppermute | solution.py:87
  46.4 12.6 %collective-permute-done.9 = bf16[72,2048]{1,0:T(8,128)(2,1)S(1)} collective-permute-done((bf16[72,2048]{1,0:T(8,128)(2,1)S(1)}, bf16[72,2048]{1,0:T(8,128)(2,1)S(1)}, u32[]{:S(2)}, u32[]{:S(2)}) %collective-permute-start.9) | collective-permute-done | bytes 294944 | tf_op jit(solution)/shard_map/ppermute | solution.py:87
  59.1 0.6 fusion.13
  59.7 4.3 %collective-permute-start.10 = (bf16[72,2048]{1,0:T(8,128)(2,1)S(1)}, bf16[72,2048]{1,0:T(8,128)(2,1)S(1)}, u32[]{:S(2)}, u32[]{:S(2)}) collective-permute-start(bf16[72,2048]{1,0:T(8,128)(2,1)S(1)} %collective-permute-done.9), channel_id=1, source_target_pairs={{4,0},{6,2},{8,4},{10,6},{12,8},{14,10},{0,12},{2,14},{5,1},{7,3},... | collective-permute-start | bytes 884744 | tf_op jit(solution)/shard_map/ppermute | solution.py:87
  64.0 0.6 fusion.7
  64.7 0.6 fusion.9
  65.3 4.1 %collective-permute-start.6 = (bf16[128,2048]{1,0:T(8,128)(2,1)S(1)}, bf16[128,2048]{1,0:T(8,128)(2,1)S(1)}, u32[]{:S(2)}, u32[]{:S(2)}) collective-permute-start(bf16[128,2048]{1,0:T(8,128)(2,1)S(1)} %collective-permute-done.5), channel_id=1, source_target_pairs={{4,0},{6,2},{8,4},{10,6},{12,8},{14,10},{0,12},{2,14},{5,1},{7,3},... | collective-permute-start | bytes 1572872 | tf_op jit(solution)/shard_map/ppermute | solution.py:87
  70.0 0.6 fusion.5
  70.6 10.6 %collective-permute-done.6 = bf16[128,2048]{1,0:T(8,128)(2,1)S(1)} collective-permute-done((bf16[128,2048]{1,0:T(8,128)(2,1)S(1)}, bf16[128,2048]{1,0:T(8,128)(2,1)S(1)}, u32[]{:S(2)}, u32[]{:S(2)}) %collective-permute-start.6) | collective-permute-done | bytes 524320 | tf_op jit(solution)/shard_map/ppermute | solution.py:87
  81.2 0.6 fusion.1
  81.9 2.1 %fusion.10 = f32[256,384]{1,0:T(8,128)S(1)} fusion(bf16[256,2048]{1,0:T(8,128)(2,1)S(1)} %constant_dynamic-update-slice_fusion.3, bf16[384,2048]{1,0:T(8,128)(2,1)} %collective-permute-done.8), kind=kOutput, calls=%fused_computation.38 | convolution fusion | flops 402653184 | bytes 3014656 | tf_op jit(solution)/shard_map/dot_general | solution.py:16
  84.0 2.0 %fusion.15 = f32[128,384]{1,0:T(8,128)S(1)} fusion(bf16[128,2048]{1,0:T(8,128)(2,1)S(1)} %collective-permute-done.5, bf16[384,2048]{1,0:T(8,128)(2,1)} %collective-permute-done.8), kind=kOutput, calls=%fused_computation.43 | convolution fusion | flops 201326592 | bytes 2293760 | tf_op jit(solution)/shard_map/dot_general | solution.py:16
  86.1 2.1 %fusion.2 = f32[256,384]{1,0:T(8,128)S(1)} fusion(bf16[256,2048]{1,0:T(8,128)(2,1)S(1)} %constant_dynamic-update-slice_fusion, bf16[384,2048]{1,0:T(8,128)(2,1)} %collective-permute-done.8), kind=kOutput, calls=%fused_computation.30 | convolution fusion | flops 402653184 | bytes 3014656 | tf_op jit(solution)/shard_map/dot_general | solution.py:16
  88.2 2.0 %fusion.6 = f32[128,384]{1,0:T(8,128)S(1)} fusion(bf16[128,2048]{1,0:T(8,128)(2,1)S(1)} %collective-permute-done.6, bf16[384,2048]{1,0:T(8,128)(2,1)} %collective-permute-done.8), kind=kOutput, calls=%fused_computation.34 | convolution fusion | flops 201326592 | bytes 2293760 | tf_op jit(solution)/shard_map/dot_general | solution.py:16
  90.3 2.0 %fusion.4 = f32[56,384]{1,0:T(8,128)S(1)} fusion(bf16[56,2048]{1,0:T(8,128)(2,1)S(1)} %collective-permute-done.14, bf16[384,2048]{1,0:T(8,128)(2,1)} %collective-permute-done.8), kind=kOutput, calls=%fused_computation.32 | convolution fusion | flops 88080384 | bytes 1888256 | tf_op jit(solution)/shard_map/dot_general | solution.py:16
  92.2 2.0 %fusion.3 = f32[72,384]{1,0:T(8,128)S(1)} fusion(bf16[72,2048]{1,0:T(8,128)(2,1)S(1)} %collective-permute-done.10, bf16[384,2048]{1,0:T(8,128)(2,1)} %collective-permute-done.8), kind=kOutput, calls=%fused_computation.31 | convolution fusion | flops 113246208 | bytes 1978368 | tf_op jit(solution)/shard_map/dot_general | solution.py:16
  94.3 0.6 collective-permute-start.11
  94.9 2.0 %fusion.11 = f32[72,384]{1,0:T(8,128)S(1)} fusion(bf16[72,2048]{1,0:T(8,128)(2,1)S(1)} %collective-permute-done.9, bf16[384,2048]{1,0:T(8,128)(2,1)} %collective-permute-done.8), kind=kOutput, calls=%fused_computation.39 | convolution fusion | flops 113246208 | bytes 1978368 | tf_op jit(solution)/shard_map/dot_general | solution.py:16
  96.9 2.0 %fusion.12 = f32[56,384]{1,0:T(8,128)S(1)} fusion(bf16[56,2048]{1,0:T(8,128)(2,1)S(1)} %collective-permute-done.13, bf16[384,2048]{1,0:T(8,128)(2,1)} %collective-permute-done.8), kind=kOutput, calls=%fused_computation.40 | convolution fusion | flops 88080384 | bytes 1888256 | tf_op jit(solution)/shard_map/dot_general | solution.py:16
  99.0 0.6 collective-permute-start.15
  99.6 0.8 collective-permute-done.18
  100.6 1.3 %collective-permute-done.22 = f32[128,384]{1,0:T(8,128)S(1)} collective-permute-done((f32[128,384]{1,0:T(8,128)S(1)}, f32[128,384]{1,0:T(8,128)S(1)}, u32[]{:S(2)}, u32[]{:S(2)}) %collective-permute-start.22) | collective-permute-done | bytes 196640 | tf_op jit(solution)/shard_map/ppermute | solution.py:90
  101.9 0.5 collective-permute-start.26
  102.5 0.5 collective-permute-start.7
  103.0 1.5 %collective-permute-start.12 = (f32[72,384]{1,0:T(8,128)S(1)}, f32[72,384]{1,0:T(8,128)S(1)}, u32[]{:S(2)}, u32[]{:S(2)}) collective-permute-start(f32[72,384]{1,0:T(8,128)S(1)} %select_add_fusion.3), channel_id=1, source_target_pairs={{0,2},{2,0},{4,6},{6,4},{8,10},{10,8},{12,14},{14,12},{1,3},{3,1},... | collective-permute-start | bytes 331784 | tf_op jit(solution)/shard_map/ppermute | solution.py:87
  104.5 0.5 collective-permute-start.19
  105.1 4.6 %collective-permute-done.26.refs_5_ = f32[128,384]{1,0:T(8,128)S(1)} collective-permute-done((f32[128,384]{1,0:T(8,128)S(1)}, f32[128,384]{1,0:T(8,128)S(1)}, u32[]{:S(2)}, u32[]{:S(2)}) %collective-permute-start.26) | collective-permute-done | bytes 196640 | tf_op jit(solution)/shard_map/ppermute | solution.py:87
  109.6 0.5 collective-permute-start.23
  110.2 9.4 %collective-permute-done.23.refs_2_ = f32[128,384]{1,0:T(8,128)S(1)} collective-permute-done((f32[128,384]{1,0:T(8,128)S(1)}, f32[128,384]{1,0:T(8,128)S(1)}, u32[]{:S(2)}, u32[]{:S(2)}) %collective-permute-start.23) | collective-permute-done | bytes 196640 | tf_op jit(solution)/shard_map/ppermute | solution.py:87
  119.6 0.5 collective-permute-start.16
  120.1 0.9 shard_map.30.refs_9_
  121.0 3.1 %collective-permute-done.16.refs_3_ = f32[56,384]{1,0:T(8,128)S(1)} collective-permute-done((f32[56,384]{1,0:T(8,128)S(1)}, f32[56,384]{1,0:T(8,128)S(1)}, u32[]{:S(2)}, u32[]{:S(2)}) %collective-permute-start.16) | collective-permute-done | bytes 86048 | tf_op jit(solution)/shard_map/ppermute | solution.py:87
  124.1 0.8 shard_map.31
  (45 shorter events, 2.1 us)
Async XLA Ops:
  1.2 20.0 %collective-permute-start.1 = (bf16[72,2048]{1,0:T(8,128)(2,1)S(1)}, bf16[72,2048]{1,0:T(8,128)(2,1)S(1)}, u32[]{:S(2)}, u32[]{:S(2)}) collective-permute-start(bf16[72,2048]{1,0:T(8,128)(2,1)S(1)} %get-tuple-element.11), channel_id=1, source_target_pairs={{0,2},{2,0},{4,6},{6,4},{8,10},{10,8},{12,14},{14,12},{1,3},{3,1},... | collective-permute-start | bytes 884744 | tf_op jit(solution)/shard_map/ppermute | solution.py:87
  4.3 12.9 %collective-permute-start.3 = (bf16[56,2048]{1,0:T(8,128)(2,1)S(1)}, bf16[56,2048]{1,0:T(8,128)(2,1)}, u32[]{:S(2)}, u32[]{:S(2)}) collective-permute-start(bf16[56,2048]{1,0:T(8,128)(2,1)S(1)} %get-tuple-element.12), channel_id=1, source_target_pairs={{0,2},{2,0},{4,6},{6,4},{8,10},{10,8},{12,14},{14,12},{1,3},{3,1},... | collective-permute-start | bytes 688136 | tf_op jit(solution)/shard_map/ppermute | solution.py:87
  7.4 74.4 %collective-permute-start.8 = (bf16[384,2048]{1,0:T(8,128)(2,1)}, bf16[384,2048]{1,0:T(8,128)(2,1)}, u32[]{:S(2)}, u32[]{:S(2)}) collective-permute-start(bf16[384,2048]{1,0:T(8,128)(2,1)} %get-tuple-element.14), channel_id=1, source_target_pairs={{0,2},{2,0},{4,6},{6,4},{8,10},{10,8},{12,14},{14,12},{1,3},{3,1},... | collective-permute-start | bytes 4718600 | tf_op jit(solution)/shard_map/ppermute | solution.py:87
  9.4 25.1 %collective-permute-start = (bf16[128,2048]{1,0:T(8,128)(2,1)S(1)}, bf16[128,2048]{1,0:T(8,128)(2,1)S(1)}, u32[]{:S(2)}, u32[]{:S(2)}) collective-permute-start(bf16[128,2048]{1,0:T(8,128)(2,1)S(1)} %get-tuple-element.10), channel_id=1, source_target_pairs={{4,0},{6,2},{8,4},{10,6},{12,8},{14,10},{0,12},{2,14},{5,1},{7,3},... | collective-permute-start | bytes 1572872 | tf_op jit(solution)/shard_map/ppermute | solution.py:87
  17.1 13.2 %collective-permute-start.4 = (bf16[56,2048]{1,0:T(8,128)(2,1)}, bf16[56,2048]{1,0:T(8,128)(2,1)S(1)}, u32[]{:S(2)}, u32[]{:S(2)}) collective-permute-start(bf16[56,2048]{1,0:T(8,128)(2,1)} %collective-permute-done.3), channel_id=1, source_target_pairs={{4,0},{6,2},{8,4},{10,6},{12,8},{14,10},{0,12},{2,14},{5,1},{7,3},... | collective-permute-start | bytes 688136 | tf_op jit(solution)/shard_map/ppermute | solution.py:87
  21.3 15.3 %collective-permute-start.2 = (bf16[72,2048]{1,0:T(8,128)(2,1)S(1)}, bf16[72,2048]{1,0:T(8,128)(2,1)S(1)}, u32[]{:S(2)}, u32[]{:S(2)}) collective-permute-start(bf16[72,2048]{1,0:T(8,128)(2,1)S(1)} %collective-permute-done.1), channel_id=1, source_target_pairs={{4,0},{6,2},{8,4},{10,6},{12,8},{14,10},{0,12},{2,14},{5,1},{7,3},... | collective-permute-start | bytes 884744 | tf_op jit(solution)/shard_map/ppermute | solution.py:87
  30.4 11.3 %collective-permute-start.13 = (bf16[56,2048]{1,0:T(8,128)(2,1)S(1)}, bf16[56,2048]{1,0:T(8,128)(2,1)S(1)}, u32[]{:S(2)}, u32[]{:S(2)}) collective-permute-start(bf16[56,2048]{1,0:T(8,128)(2,1)S(1)} %collective-permute-done.4), channel_id=1, source_target_pairs={{4,0},{6,2},{8,4},{10,6},{12,8},{14,10},{0,12},{2,14},{5,1},{7,3},... | collective-permute-start | bytes 688136 | tf_op jit(solution)/shard_map/ppermute | solution.py:87
  34.5 30.1 %collective-permute-start.5 = (bf16[128,2048]{1,0:T(8,128)(2,1)S(1)}, bf16[128,2048]{1,0:T(8,128)(2,1)S(1)}, u32[]{:S(2)}, u32[]{:S(2)}) collective-permute-start(bf16[128,2048]{1,0:T(8,128)(2,1)S(1)} %collective-permute-done), channel_id=1, source_target_pairs={{4,0},{6,2},{8,4},{10,6},{12,8},{14,10},{0,12},{2,14},{5,1},{7,3},... | collective-permute-start | bytes 1572872 | tf_op jit(solution)/shard_map/ppermute | solution.py:87
  36.6 22.5 %collective-permute-start.9 = (bf16[72,2048]{1,0:T(8,128)(2,1)S(1)}, bf16[72,2048]{1,0:T(8,128)(2,1)S(1)}, u32[]{:S(2)}, u32[]{:S(2)}) collective-permute-start(bf16[72,2048]{1,0:T(8,128)(2,1)S(1)} %collective-permute-done.2), channel_id=1, source_target_pairs={{4,0},{6,2},{8,4},{10,6},{12,8},{14,10},{0,12},{2,14},{5,1},{7,3},... | collective-permute-start | bytes 884744 | tf_op jit(solution)/shard_map/ppermute | solution.py:87
  42.2 21.8 %collective-permute-start.14 = (bf16[56,2048]{1,0:T(8,128)(2,1)S(1)}, bf16[56,2048]{1,0:T(8,128)(2,1)S(1)}, u32[]{:S(2)}, u32[]{:S(2)}) collective-permute-start(bf16[56,2048]{1,0:T(8,128)(2,1)S(1)} %collective-permute-done.13), channel_id=1, source_target_pairs={{4,0},{6,2},{8,4},{10,6},{12,8},{14,10},{0,12},{2,14},{5,1},{7,3},... | collective-permute-start | bytes 688136 | tf_op jit(solution)/shard_map/ppermute | solution.py:87
  59.7 10.0 %collective-permute-start.10 = (bf16[72,2048]{1,0:T(8,128)(2,1)S(1)}, bf16[72,2048]{1,0:T(8,128)(2,1)S(1)}, u32[]{:S(2)}, u32[]{:S(2)}) collective-permute-start(bf16[72,2048]{1,0:T(8,128)(2,1)S(1)} %collective-permute-done.9), channel_id=1, source_target_pairs={{4,0},{6,2},{8,4},{10,6},{12,8},{14,10},{0,12},{2,14},{5,1},{7,3},... | collective-permute-start | bytes 884744 | tf_op jit(solution)/shard_map/ppermute | solution.py:87
  64.6 37.8 %collective-permute-start.20 = (f32[56,384]{1,0:T(8,128)S(1)}, f32[56,384]{1,0:T(8,128)S(1)}, u32[]{:S(2)}, u32[]{:S(2)}) collective-permute-start(f32[56,384]{1,0:T(8,128)S(1)} %get-tuple-element.23), channel_id=1, source_target_pairs={{0,1},{1,0},{2,3},{3,2},{4,5},{5,4},{6,7},{7,6},{8,9},{9,8},{10,11... | collective-permute-start | bytes 258056 | tf_op jit(solution)/shard_map/ppermute | solution.py:90
  65.3 15.9 %collective-permute-start.6 = (bf16[128,2048]{1,0:T(8,128)(2,1)S(1)}, bf16[128,2048]{1,0:T(8,128)(2,1)S(1)}, u32[]{:S(2)}, u32[]{:S(2)}) collective-permute-start(bf16[128,2048]{1,0:T(8,128)(2,1)S(1)} %collective-permute-done.5), channel_id=1, source_target_pairs={{4,0},{6,2},{8,4},{10,6},{12,8},{14,10},{0,12},{2,14},{5,1},{7,3},... | collective-permute-start | bytes 1572872 | tf_op jit(solution)/shard_map/ppermute | solution.py:87
  69.4 33.1 %collective-permute-start.21 = (f32[128,384]{1,0:T(8,128)S(1)}, f32[128,384]{1,0:T(8,128)S(1)}, u32[]{:S(2)}, u32[]{:S(2)}) collective-permute-start(f32[128,384]{1,0:T(8,128)S(1)} %get-tuple-element.28), channel_id=1, source_target_pairs={{0,1},{1,0},{2,3},{3,2},{4,5},{5,4},{6,7},{7,6},{8,9},{9,8},{10,11... | collective-permute-start | bytes 589832 | tf_op jit(solution)/shard_map/ppermute | solution.py:90
  69.7 33.3 %collective-permute-start.24 = (f32[128,384]{1,0:T(8,128)S(1)}, f32[128,384]{1,0:T(8,128)S(1)}, u32[]{:S(2)}, u32[]{:S(2)}) collective-permute-start(f32[128,384]{1,0:T(8,128)S(1)} %get-tuple-element.15), channel_id=1, source_target_pairs={{0,1},{1,0},{2,3},{3,2},{4,5},{5,4},{6,7},{7,6},{8,9},{9,8},{10,11... | collective-permute-start | bytes 589832 | tf_op jit(solution)/shard_map/ppermute | solution.py:90
  86.0 13.0 %collective-permute-start.25 = (f32[128,384]{1,0:T(8,128)S(1)}, f32[128,384]{1,0:T(8,128)S(1)}, u32[]{:S(2)}, u32[]{:S(2)}) collective-permute-start(f32[128,384]{1,0:T(8,128)S(1)} %slice_select_fusion), channel_id=1, source_target_pairs={{0,1},{1,0},{2,3},{3,2},{4,5},{5,4},{6,7},{7,6},{8,9},{9,8},{10,11... | collective-permute-start | bytes 589832 | tf_op jit(solution)/shard_map/ppermute | solution.py:90
  94.3 4.6 %collective-permute-start.11 = (f32[72,384]{1,0:T(8,128)S(1)}, f32[72,384]{1,0:T(8,128)S(1)}, u32[]{:S(2)}, u32[]{:S(2)}) collective-permute-start(f32[72,384]{1,0:T(8,128)S(1)} %slice_select_fusion.11), channel_id=1, source_target_pairs={{0,1},{1,0},{2,3},{3,2},{4,5},{5,4},{6,7},{7,6},{8,9},{9,8},{10,11... | collective-permute-start | bytes 331784 | tf_op jit(solution)/shard_map/ppermute | solution.py:90
  98.9 1.5 %collective-permute-start.18 = (f32[128,384]{1,0:T(8,128)S(1)}, f32[128,384]{1,0:T(8,128)S(1)}, u32[]{:S(2)}, u32[]{:S(2)}) collective-permute-start(f32[128,384]{1,0:T(8,128)S(1)} %slice_select_fusion.6), channel_id=1, source_target_pairs={{0,1},{1,0},{2,3},{3,2},{4,5},{5,4},{6,7},{7,6},{8,9},{9,8},{10,11... | collective-permute-start | bytes 589832 | tf_op jit(solution)/shard_map/ppermute | solution.py:90
  99.0 5.5 %collective-permute-start.15 = (f32[56,384]{1,0:T(8,128)S(1)}, f32[56,384]{1,0:T(8,128)S(1)}, u32[]{:S(2)}, u32[]{:S(2)}) collective-permute-start(f32[56,384]{1,0:T(8,128)S(1)} %slice_select_fusion.14), channel_id=1, source_target_pairs={{0,1},{1,0},{2,3},{3,2},{4,5},{5,4},{6,7},{7,6},{8,9},{9,8},{10,11... | collective-permute-start | bytes 258056 | tf_op jit(solution)/shard_map/ppermute | solution.py:90
  100.4 1.4 %collective-permute-start.22 = (f32[128,384]{1,0:T(8,128)S(1)}, f32[128,384]{1,0:T(8,128)S(1)}, u32[]{:S(2)}, u32[]{:S(2)}) collective-permute-start(f32[128,384]{1,0:T(8,128)S(1)} %get-tuple-element.26), channel_id=1, source_target_pairs={{0,1},{1,0},{2,3},{3,2},{4,5},{5,4},{6,7},{7,6},{8,9},{9,8},{10,11... | collective-permute-start | bytes 589832 | tf_op jit(solution)/shard_map/ppermute | solution.py:90
  101.9 7.8 %collective-permute-start.26 = (f32[128,384]{1,0:T(8,128)S(1)}, f32[128,384]{1,0:T(8,128)S(1)}, u32[]{:S(2)}, u32[]{:S(2)}) collective-permute-start(f32[128,384]{1,0:T(8,128)S(1)} %get-tuple-element.25), channel_id=1, source_target_pairs={{0,2},{2,0},{4,6},{6,4},{8,10},{10,8},{12,14},{14,12},{1,3},{3,1},... | collective-permute-start | bytes 589832 | tf_op jit(solution)/shard_map/ppermute | solution.py:87
  102.4 18.6 %collective-permute-start.17 = (f32[72,384]{1,0:T(8,128)S(1)}, f32[72,384]{1,0:T(8,128)S(1)}, u32[]{:S(2)}, u32[]{:S(2)}) collective-permute-start(f32[72,384]{1,0:T(8,128)S(1)} %get-tuple-element.21), channel_id=1, source_target_pairs={{0,1},{1,0},{2,3},{3,2},{4,5},{5,4},{6,7},{7,6},{8,9},{9,8},{10,11... | collective-permute-start | bytes 331784 | tf_op jit(solution)/shard_map/ppermute | solution.py:90
  102.5 21.6 %collective-permute-start.7 = (f32[128,384]{1,0:T(8,128)S(1)}, f32[128,384]{1,0:T(8,128)S(1)}, u32[]{:S(2)}, u32[]{:S(2)}) collective-permute-start(f32[128,384]{1,0:T(8,128)S(1)} %get-tuple-element.19), channel_id=1, source_target_pairs={{0,1},{1,0},{2,3},{3,2},{4,5},{5,4},{6,7},{7,6},{8,9},{9,8},{10,11... | collective-permute-start | bytes 589832 | tf_op jit(solution)/shard_map/ppermute | solution.py:90
  103.0 21.1 %collective-permute-start.12 = (f32[72,384]{1,0:T(8,128)S(1)}, f32[72,384]{1,0:T(8,128)S(1)}, u32[]{:S(2)}, u32[]{:S(2)}) collective-permute-start(f32[72,384]{1,0:T(8,128)S(1)} %select_add_fusion.3), channel_id=1, source_target_pairs={{0,2},{2,0},{4,6},{6,4},{8,10},{10,8},{12,14},{14,12},{1,3},{3,1},... | collective-permute-start | bytes 331784 | tf_op jit(solution)/shard_map/ppermute | solution.py:87
  104.5 19.6 %collective-permute-start.19 = (f32[128,384]{1,0:T(8,128)S(1)}, f32[128,384]{1,0:T(8,128)S(1)}, u32[]{:S(2)}, u32[]{:S(2)}) collective-permute-start(f32[128,384]{1,0:T(8,128)S(1)} %select_add_fusion.2), channel_id=1, source_target_pairs={{0,2},{2,0},{4,6},{6,4},{8,10},{10,8},{12,14},{14,12},{1,3},{3,1},... | collective-permute-start | bytes 589832 | tf_op jit(solution)/shard_map/ppermute | solution.py:87
  109.6 10.0 %collective-permute-start.23 = (f32[128,384]{1,0:T(8,128)S(1)}, f32[128,384]{1,0:T(8,128)S(1)}, u32[]{:S(2)}, u32[]{:S(2)}) collective-permute-start(f32[128,384]{1,0:T(8,128)S(1)} %select_add_fusion.1), channel_id=1, source_target_pairs={{0,2},{2,0},{4,6},{6,4},{8,10},{10,8},{12,14},{14,12},{1,3},{3,1},... | collective-permute-start | bytes 589832 | tf_op jit(solution)/shard_map/ppermute | solution.py:87
  119.6 4.5 %collective-permute-start.16 = (f32[56,384]{1,0:T(8,128)S(1)}, f32[56,384]{1,0:T(8,128)S(1)}, u32[]{:S(2)}, u32[]{:S(2)}) collective-permute-start(f32[56,384]{1,0:T(8,128)S(1)} %select_add_fusion.4), channel_id=1, source_target_pairs={{0,2},{2,0},{4,6},{6,4},{8,10},{10,8},{12,14},{14,12},{1,3},{3,1},... | collective-permute-start | bytes 258056 | tf_op jit(solution)/shard_map/ppermute | solution.py:87

commit v5 on v4

--- a/solution.py
+++ b/solution.py
@@ -89,7 +89,7 @@
     def cores(value):
         return lax.ppermute(value, "layers", [(0, 1), (1, 0)])
 
-    cut = size * 9 // 16
+    cut = size * 5 // 8
     rest = size - cut
     held, given_b, given_c = parted(row, queries, (cut,))
     firsts = {"A": held, "B": move(given_b, swap), "C": move(given_c, swap)}
@@ -98,8 +98,10 @@
     heights = {"A": size, "B": cut, "C": rest}
     starts = {"A": 0, "B": size, "C": size + cut}
     held_at = [firsts]
-    for _ in range(1, count):
-        held_at.append({piece: move(value, ring) for piece, value in held_at[-1].items()})
+    back = [(target, source) for source, target in ring]
+    for step in range(1, count):
+        hops, values = (ring, held_at[-1]) if step < count - 1 else (back, firsts)
+        held_at.append({piece: move(value, hops) for piece, value in values.items()})
 
     def score(value, side):
         return lax.optimization_barrier(product(value, sides[side]))
@@ -107,7 +109,7 @@
     partial = {}
     for step, values in enumerate(held_at):
         for side in sides:
-            if step < half:
+            if step != half:
                 whole = score(jnp.concatenate(list(values.values())), side)
                 for piece in values:
                     first = starts[piece]
@@ -117,10 +119,10 @@
                     partial[side, piece, step] = score(value, side)
 
     total = None
-    for group in range(half):
+    for group in reversed(range(half)):
         mine = lax.rem(z + group, count) // half == core
         sums, crossed = {}, {}
-        for pieces in ("A", "BC") if group < half - 1 else "ABC":
+        for pieces in ("A", "BC") if group else "ABC":
             for side in "NO":
                 one, two = [
                     jnp.concatenate([partial[side, piece, step] for piece in pieces]) for step in (group, group + half)

time: 125 us -> 122 us (0.976)
  waiting for transfers between devices: 55.3 us -> 66.7 us
  starting transfers between devices: 40.6 us -> 29.7 us
  matrix products: 21.2 us -> 16.5 us
    ppermute x17, starting transfers between devices: 38 us -> 27.7 us  [move(): return lax.ppermute(value, 'rows', hops)]
    ppermute x17, waiting for transfers between devices: 53.2 us -> 61.7 us  [move(): return lax.ppermute(value, 'rows', hops)]
    dot_general x16 -> x12, matrix products: 21.2 us -> 16.5 us  [product(): return lax.dot_general(left, right, NT, preferred_element_type=jnp.float32)]
    ppermute x10, waiting for transfers between devices: 2.06 us -> 5.04 us  [cores(): return lax.ppermute(value, 'layers', [(0, 1), (1, 0)])]
  transfers between devices with their start and end apart: 27 -> 27, of which waited for: 10 -> 11; matrix products, arithmetic and copies ran while one was open for 18% -> 16% of each run, Pallas kernels for 3% -> 3%
where the time goes in v5:
time: 122 us
  waiting for transfers between devices  66.7 us (55%)
  starting transfers between devices  29.7 us (24%)
  matrix products  16.5 us (14%)
  Pallas kernels  5.97 us (5%)
  local copies, waits for them, and re-layouts  2.2 us (2%)
    ppermute x17, waiting for transfers between devices, move(): return lax.ppermute(value, 'rows', hops)  61.7 us
    ppermute x17, starting transfers between devices, move(): return lax.ppermute(value, 'rows', hops)  27.7 us
    dot_general x12, matrix products, product(): return lax.dot_general(left, right, NT, preferred_element_type=jnp.float32)  16.5 us
    ppermute x10, waiting for transfers between devices, cores(): return lax.ppermute(value, 'layers', [(0, 1), (1, 0)])  5.04 us
    pallas_call x2, Pallas kernels, parted(): pl.pallas_call(functools.partial(part, spans), out_shape=[pltpu.VMEM(shap...  4.29 us
  transfers between devices with their start and end apart: 27, of which 11 were waited for; matrix products, arithmetic and copies ran while one was open for 16% of the time, Pallas kernels for 3%

profile of v5, /device:TPU:0, one launch (start us, length us, event | category | flops | bytes accessed | tf_op | source)
XLA Modules:
  0.0 121.7 jit_solution(16941539875313248856)
XLA Ops:
  0.0 1.2 shard_map.28
  1.2 3.0 %collective-permute-start = (bf16[80,2048]{1,0:T(8,128)(2,1)S(1)}, bf16[80,2048]{1,0:T(8,128)(2,1)S(1)}, u32[]{:S(2)}, u32[]{:S(2)}) collective-permute-start(bf16[80,2048]{1,0:T(8,128)(2,1)S(1)} %get-tuple-element.11), channel_id=1, source_target_pairs={{0,2},{2,0},{4,6},{6,4},{8,10},{10,8},{12,14},{14,12},{1,3},{3,1},... | collective-permute-start | bytes 983048 | tf_op jit(solution)/shard_map/ppermute | solution.py:87
  4.2 1.6 %collective-permute-start.18 = (bf16[128,2048]{1,0:T(8,128)(2,1)S(1)}, bf16[128,2048]{1,0:T(8,128)(2,1)}, u32[]{:S(2)}, u32[]{:S(2)}) collective-permute-start(bf16[128,2048]{1,0:T(8,128)(2,1)S(1)} %get-tuple-element.10), channel_id=1, source_target_pairs={{0,4},{2,6},{4,8},{6,10},{8,12},{10,14},{12,0},{14,2},{1,5},{3,7},... | collective-permute-start | bytes 1572872 | tf_op jit(solution)/shard_map/ppermute | solution.py:87
  5.8 2.2 %collective-permute-start.2 = (bf16[128,2048]{1,0:T(8,128)(2,1)S(1)}, bf16[128,2048]{1,0:T(8,128)(2,1)S(1)}, u32[]{:S(2)}, u32[]{:S(2)}) collective-permute-start(bf16[128,2048]{1,0:T(8,128)(2,1)S(1)} %get-tuple-element.10), channel_id=1, source_target_pairs={{4,0},{6,2},{8,4},{10,6},{12,8},{14,10},{0,12},{2,14},{5,1},{7,3},... | collective-permute-start | bytes 1572872 | tf_op jit(solution)/shard_map/ppermute | solution.py:87
  8.1 0.3 collective-permute-start.1
  8.4 3.1 %shard_map.29 = (bf16[384,2048]{1,0:T(8,128)(2,1)S(1)}, bf16[384,2048]{1,0:T(8,128)(2,1)}) custom-call(s32[1]{0:T(128)} %bitcast.row_ref, bf16[384,4096]{1,0:T(8,128)(2,1)} %bitcast.27), custom_call_target="tpu_custom_call" | custom-call | tf_op jit(solution)/shard_map/pallas_call | solution.py:64
  11.5 1.8 %collective-permute-start.5 = (bf16[384,2048]{1,0:T(8,128)(2,1)}, bf16[384,2048]{1,0:T(8,128)(2,1)}, u32[]{:S(2)}, u32[]{:S(2)}) collective-permute-start(bf16[384,2048]{1,0:T(8,128)(2,1)} %get-tuple-element.14), channel_id=1, source_target_pairs={{0,2},{2,0},{4,6},{6,4},{8,10},{10,8},{12,14},{14,12},{1,3},{3,1},... | collective-permute-start | bytes 4718600 | tf_op jit(solution)/shard_map/ppermute | solution.py:87
  13.3 3.8 %collective-permute-done.1 = bf16[48,2048]{1,0:T(8,128)(2,1)} collective-permute-done((bf16[48,2048]{1,0:T(8,128)(2,1)S(1)}, bf16[48,2048]{1,0:T(8,128)(2,1)}, u32[]{:S(2)}, u32[]{:S(2)}) %collective-permute-start.1) | collective-permute-done | bytes 196640 | tf_op jit(solution)/shard_map/ppermute | solution.py:87
  17.1 2.1 %collective-permute-start.20 = (bf16[48,2048]{1,0:T(8,128)(2,1)}, bf16[48,2048]{1,0:T(8,128)(2,1)S(1)}, u32[]{:S(2)}, u32[]{:S(2)}) collective-permute-start(bf16[48,2048]{1,0:T(8,128)(2,1)} %collective-permute-done.1), channel_id=1, source_target_pairs={{0,4},{2,6},{4,8},{6,10},{8,12},{10,14},{12,0},{14,2},{1,5},{3,7},... | collective-permute-start | bytes 589832 | tf_op jit(solution)/shard_map/ppermute | solution.py:87
  19.2 2.0 %collective-permute-start.10 = (bf16[48,2048]{1,0:T(8,128)(2,1)}, bf16[48,2048]{1,0:T(8,128)(2,1)S(1)}, u32[]{:S(2)}, u32[]{:S(2)}) collective-permute-start(bf16[48,2048]{1,0:T(8,128)(2,1)} %collective-permute-done.1), channel_id=1, source_target_pairs={{4,0},{6,2},{8,4},{10,6},{12,8},{14,10},{0,12},{2,14},{5,1},{7,3},... | collective-permute-start | bytes 589832 | tf_op jit(solution)/shard_map/ppermute | solution.py:87
  21.3 0.9 constant_dynamic-update-slice_fusion
  22.2 0.7 fusion
  23.0 5.5 %collective-permute-start.19 = (bf16[80,2048]{1,0:T(8,128)(2,1)S(1)}, bf16[80,2048]{1,0:T(8,128)(2,1)S(1)}, u32[]{:S(2)}, u32[]{:S(2)}) collective-permute-start(bf16[80,2048]{1,0:T(8,128)(2,1)S(1)} %collective-permute-done), channel_id=1, source_target_pairs={{0,4},{2,6},{4,8},{6,10},{8,12},{10,14},{12,0},{14,2},{1,5},{3,7},... | collective-permute-start | bytes 983048 | tf_op jit(solution)/shard_map/ppermute | solution.py:87
  28.5 1.1 constant_dynamic-update-slice_fusion.8
  29.6 9.7 %collective-permute-done.10 = bf16[48,2048]{1,0:T(8,128)(2,1)S(1)} collective-permute-done((bf16[48,2048]{1,0:T(8,128)(2,1)}, bf16[48,2048]{1,0:T(8,128)(2,1)S(1)}, u32[]{:S(2)}, u32[]{:S(2)}) %collective-permute-start.10) | collective-permute-done | bytes 196640 | tf_op jit(solution)/shard_map/ppermute | solution.py:87
  39.3 2.9 %collective-permute-start.6 = (bf16[80,2048]{1,0:T(8,128)(2,1)S(1)}, bf16[80,2048]{1,0:T(8,128)(2,1)S(1)}, u32[]{:S(2)}, u32[]{:S(2)}) collective-permute-start(bf16[80,2048]{1,0:T(8,128)(2,1)S(1)} %collective-permute-done), channel_id=1, source_target_pairs={{4,0},{6,2},{8,4},{10,6},{12,8},{14,10},{0,12},{2,14},{5,1},{7,3},... | collective-permute-start | bytes 983048 | tf_op jit(solution)/shard_map/ppermute | solution.py:87
  42.2 0.4 collective-permute-start.11
  42.7 14.8 %collective-permute-done.11 = bf16[48,2048]{1,0:T(8,128)(2,1)S(1)} collective-permute-done((bf16[48,2048]{1,0:T(8,128)(2,1)S(1)}, bf16[48,2048]{1,0:T(8,128)(2,1)S(1)}, u32[]{:S(2)}, u32[]{:S(2)}) %collective-permute-start.11) | collective-permute-done | bytes 196640 | tf_op jit(solution)/shard_map/ppermute | solution.py:87
  57.5 1.6 %collective-permute-start.3 = (bf16[128,2048]{1,0:T(8,128)(2,1)S(1)}, bf16[128,2048]{1,0:T(8,128)(2,1)S(1)}, u32[]{:S(2)}, u32[]{:S(2)}) collective-permute-start(bf16[128,2048]{1,0:T(8,128)(2,1)S(1)} %collective-permute-done.2), channel_id=1, source_target_pairs={{4,0},{6,2},{8,4},{10,6},{12,8},{14,10},{0,12},{2,14},{5,1},{7,3},... | collective-permute-start | bytes 1572872 | tf_op jit(solution)/shard_map/ppermute | solution.py:87
  59.1 0.6 fusion.7
  59.9 0.7 fusion.9
  60.6 0.5 collective-permute-start.7
  61.2 0.7 fusion.8
  62.3 16.1 %collective-permute-done.7 = bf16[80,2048]{1,0:T(8,128)(2,1)S(1)} collective-permute-done((bf16[80,2048]{1,0:T(8,128)(2,1)S(1)}, bf16[80,2048]{1,0:T(8,128)(2,1)S(1)}, u32[]{:S(2)}, u32[]{:S(2)}) %collective-permute-start.7) | collective-permute-done | bytes 327712 | tf_op jit(solution)/shard_map/ppermute | solution.py:87
  78.4 0.6 fusion.5
  79.0 0.6 fusion.1
  79.7 2.2 %fusion.2 = f32[256,384]{1,0:T(8,128)S(1)} fusion(bf16[256,2048]{1,0:T(8,128)(2,1)S(1)} %constant_dynamic-update-slice_fusion, bf16[384,2048]{1,0:T(8,128)(2,1)} %collective-permute-done.5), kind=kOutput, calls=%fused_computation.31 | convolution fusion | flops 402653184 | bytes 3014656 | tf_op jit(solution)/shard_map/dot_general | solution.py:16
  81.8 2.2 %fusion.10 = f32[256,384]{1,0:T(8,128)S(1)} fusion(bf16[256,2048]{1,0:T(8,128)(2,1)S(1)} %constant_dynamic-update-slice_fusion.3, bf16[384,2048]{1,0:T(8,128)(2,1)} %collective-permute-done.5), kind=kOutput, calls=%fused_computation.39 | convolution fusion | flops 402653184 | bytes 3014656 | tf_op jit(solution)/shard_map/dot_general | solution.py:16
  84.0 2.2 %fusion.11 = f32[256,384]{1,0:T(8,128)S(1)} fusion(bf16[256,2048]{1,0:T(8,128)(2,1)S(1)} %constant_dynamic-update-slice_fusion.6, bf16[384,2048]{1,0:T(8,128)(2,1)} %collective-permute-done.5), kind=kOutput, calls=%fused_computation.40 | convolution fusion | flops 402653184 | bytes 3014656 | tf_op jit(solution)/shard_map/dot_general | solution.py:16
  86.2 2.0 %fusion.4 = f32[48,384]{1,0:T(8,128)S(1)} fusion(bf16[48,2048]{1,0:T(8,128)(2,1)S(1)} %collective-permute-done.11, bf16[384,2048]{1,0:T(8,128)(2,1)} %collective-permute-done.5), kind=kOutput, calls=%fused_computation.33 | convolution fusion | flops 75497472 | bytes 1843200 | tf_op jit(solution)/shard_map/dot_general | solution.py:16
  88.2 2.0 %fusion.3 = f32[80,384]{1,0:T(8,128)S(1)} fusion(bf16[80,2048]{1,0:T(8,128)(2,1)S(1)} %collective-permute-done.7, bf16[384,2048]{1,0:T(8,128)(2,1)} %collective-permute-done.5), kind=kOutput, calls=%fused_computation.32 | convolution fusion | flops 125829120 | bytes 2023424 | tf_op jit(solution)/shard_map/dot_general | solution.py:16
  90.2 2.0 %fusion.6 = f32[128,384]{1,0:T(8,128)S(1)} fusion(bf16[128,2048]{1,0:T(8,128)(2,1)S(1)} %collective-permute-done.3, bf16[384,2048]{1,0:T(8,128)(2,1)} %collective-permute-done.5), kind=kOutput, calls=%fused_computation.35 | convolution fusion | flops 201326592 | bytes 2293760 | tf_op jit(solution)/shard_map/dot_general | solution.py:16
  92.2 0.6 collective-permute-start.12
  92.9 1.3 %collective-permute-done.8 = f32[80,384]{1,0:T(8,128)S(1)} collective-permute-done((f32[80,384]{1,0:T(8,128)S(1)}, f32[80,384]{1,0:T(8,128)S(1)}, u32[]{:S(2)}, u32[]{:S(2)}) %collective-permute-start.8) | collective-permute-done | bytes 122912 | tf_op jit(solution)/shard_map/ppermute | solution.py:90
  94.4 1.3 %collective-permute-done.25 = f32[128,384]{1,0:T(8,128)S(1)} collective-permute-done((f32[128,384]{1,0:T(8,128)S(1)}, f32[128,384]{1,0:T(8,128)S(1)}, u32[]{:S(2)}, u32[]{:S(2)}) %collective-permute-start.25) | collective-permute-done | bytes 196640 | tf_op jit(solution)/shard_map/ppermute | solution.py:90
  95.8 1.2 %collective-permute-done.15 = f32[128,384]{1,0:T(8,128)S(1)} collective-permute-done((f32[128,384]{1,0:T(8,128)S(1)}, f32[128,384]{1,0:T(8,128)S(1)}, u32[]{:S(2)}, u32[]{:S(2)}) %collective-permute-start.15) | collective-permute-done | bytes 196640 | tf_op jit(solution)/shard_map/ppermute | solution.py:90
  97.3 1.3 %collective-permute-done.22 = f32[128,384]{1,0:T(8,128)S(1)} collective-permute-done((f32[128,384]{1,0:T(8,128)S(1)}, f32[128,384]{1,0:T(8,128)S(1)}, u32[]{:S(2)}, u32[]{:S(2)}) %collective-permute-start.22) | collective-permute-done | bytes 196640 | tf_op jit(solution)/shard_map/ppermute | solution.py:90
  98.5 0.5 collective-permute-start.26
  99.2 0.5 collective-permute-start.4
  99.7 1.5 %collective-permute-start.9 = (f32[80,384]{1,0:T(8,128)S(1)}, f32[80,384]{1,0:T(8,128)S(1)}, u32[]{:S(2)}, u32[]{:S(2)}) collective-permute-start(f32[80,384]{1,0:T(8,128)S(1)} %select_add_fusion.3), channel_id=1, source_target_pairs={{0,2},{2,0},{4,6},{6,4},{8,10},{10,8},{12,14},{14,12},{1,3},{3,1},... | collective-permute-start | bytes 368648 | tf_op jit(solution)/shard_map/ppermute | solution.py:87
  101.2 0.5 collective-permute-start.16
  101.7 4.6 %collective-permute-done.26.refs_5_ = f32[128,384]{1,0:T(8,128)S(1)} collective-permute-done((f32[128,384]{1,0:T(8,128)S(1)}, f32[128,384]{1,0:T(8,128)S(1)}, u32[]{:S(2)}, u32[]{:S(2)}) %collective-permute-start.26) | collective-permute-done | bytes 196640 | tf_op jit(solution)/shard_map/ppermute | solution.py:87
  106.3 0.5 collective-permute-start.23
  106.9 9.7 %collective-permute-done.23.refs_2_ = f32[128,384]{1,0:T(8,128)S(1)} collective-permute-done((f32[128,384]{1,0:T(8,128)S(1)}, f32[128,384]{1,0:T(8,128)S(1)}, u32[]{:S(2)}, u32[]{:S(2)}) %collective-permute-start.23) | collective-permute-done | bytes 196640 | tf_op jit(solution)/shard_map/ppermute | solution.py:87
  116.5 0.5 collective-permute-start.13
  117.1 0.9 shard_map.30.refs_9_
  118.0 2.9 %collective-permute-done.13.refs_3_ = f32[48,384]{1,0:T(8,128)S(1)} collective-permute-done((f32[48,384]{1,0:T(8,128)S(1)}, f32[48,384]{1,0:T(8,128)S(1)}, u32[]{:S(2)}, u32[]{:S(2)}) %collective-permute-start.13) | collective-permute-done | bytes 73760 | tf_op jit(solution)/shard_map/ppermute | solution.py:87
  120.9 0.8 shard_map.31
  (44 shorter events, 1.5 us)
Async XLA Ops:
  1.2 18.0 %collective-permute-start = (bf16[80,2048]{1,0:T(8,128)(2,1)S(1)}, bf16[80,2048]{1,0:T(8,128)(2,1)S(1)}, u32[]{:S(2)}, u32[]{:S(2)}) collective-permute-start(bf16[80,2048]{1,0:T(8,128)(2,1)S(1)} %get-tuple-element.11), channel_id=1, source_target_pairs={{0,2},{2,0},{4,6},{6,4},{8,10},{10,8},{12,14},{14,12},{1,3},{3,1},... | collective-permute-start | bytes 983048 | tf_op jit(solution)/shard_map/ppermute | solution.py:87
  4.2 18.7 %collective-permute-start.18 = (bf16[128,2048]{1,0:T(8,128)(2,1)S(1)}, bf16[128,2048]{1,0:T(8,128)(2,1)}, u32[]{:S(2)}, u32[]{:S(2)}) collective-permute-start(bf16[128,2048]{1,0:T(8,128)(2,1)S(1)} %get-tuple-element.10), channel_id=1, source_target_pairs={{0,4},{2,6},{4,8},{6,10},{8,12},{10,14},{12,0},{14,2},{1,5},{3,7},... | collective-permute-start | bytes 1572872 | tf_op jit(solution)/shard_map/ppermute | solution.py:87
  5.8 36.4 %collective-permute-start.2 = (bf16[128,2048]{1,0:T(8,128)(2,1)S(1)}, bf16[128,2048]{1,0:T(8,128)(2,1)S(1)}, u32[]{:S(2)}, u32[]{:S(2)}) collective-permute-start(bf16[128,2048]{1,0:T(8,128)(2,1)S(1)} %get-tuple-element.10), channel_id=1, source_target_pairs={{4,0},{6,2},{8,4},{10,6},{12,8},{14,10},{0,12},{2,14},{5,1},{7,3},... | collective-permute-start | bytes 1572872 | tf_op jit(solution)/shard_map/ppermute | solution.py:87
  8.1 9.1 %collective-permute-start.1 = (bf16[48,2048]{1,0:T(8,128)(2,1)S(1)}, bf16[48,2048]{1,0:T(8,128)(2,1)}, u32[]{:S(2)}, u32[]{:S(2)}) collective-permute-start(bf16[48,2048]{1,0:T(8,128)(2,1)S(1)} %get-tuple-element.12), channel_id=1, source_target_pairs={{0,2},{2,0},{4,6},{6,4},{8,10},{10,8},{12,14},{14,12},{1,3},{3,1},... | collective-permute-start | bytes 589832 | tf_op jit(solution)/shard_map/ppermute | solution.py:87
  11.5 68.2 %collective-permute-start.5 = (bf16[384,2048]{1,0:T(8,128)(2,1)}, bf16[384,2048]{1,0:T(8,128)(2,1)}, u32[]{:S(2)}, u32[]{:S(2)}) collective-permute-start(bf16[384,2048]{1,0:T(8,128)(2,1)} %get-tuple-element.14), channel_id=1, source_target_pairs={{0,2},{2,0},{4,6},{6,4},{8,10},{10,8},{12,14},{14,12},{1,3},{3,1},... | collective-permute-start | bytes 4718600 | tf_op jit(solution)/shard_map/ppermute | solution.py:87
  17.1 42.7 %collective-permute-start.20 = (bf16[48,2048]{1,0:T(8,128)(2,1)}, bf16[48,2048]{1,0:T(8,128)(2,1)S(1)}, u32[]{:S(2)}, u32[]{:S(2)}) collective-permute-start(bf16[48,2048]{1,0:T(8,128)(2,1)} %collective-permute-done.1), channel_id=1, source_target_pairs={{0,4},{2,6},{4,8},{6,10},{8,12},{10,14},{12,0},{14,2},{1,5},{3,7},... | collective-permute-start | bytes 589832 | tf_op jit(solution)/shard_map/ppermute | solution.py:87
  19.2 20.1 %collective-permute-start.10 = (bf16[48,2048]{1,0:T(8,128)(2,1)}, bf16[48,2048]{1,0:T(8,128)(2,1)S(1)}, u32[]{:S(2)}, u32[]{:S(2)}) collective-permute-start(bf16[48,2048]{1,0:T(8,128)(2,1)} %collective-permute-done.1), channel_id=1, source_target_pairs={{4,0},{6,2},{8,4},{10,6},{12,8},{14,10},{0,12},{2,14},{5,1},{7,3},... | collective-permute-start | bytes 589832 | tf_op jit(solution)/shard_map/ppermute | solution.py:87
  23.0 36.7 %collective-permute-start.19 = (bf16[80,2048]{1,0:T(8,128)(2,1)S(1)}, bf16[80,2048]{1,0:T(8,128)(2,1)S(1)}, u32[]{:S(2)}, u32[]{:S(2)}) collective-permute-start(bf16[80,2048]{1,0:T(8,128)(2,1)S(1)} %collective-permute-done), channel_id=1, source_target_pairs={{0,4},{2,6},{4,8},{6,10},{8,12},{10,14},{12,0},{14,2},{1,5},{3,7},... | collective-permute-start | bytes 983048 | tf_op jit(solution)/shard_map/ppermute | solution.py:87
  39.3 21.3 %collective-permute-start.6 = (bf16[80,2048]{1,0:T(8,128)(2,1)S(1)}, bf16[80,2048]{1,0:T(8,128)(2,1)S(1)}, u32[]{:S(2)}, u32[]{:S(2)}) collective-permute-start(bf16[80,2048]{1,0:T(8,128)(2,1)S(1)} %collective-permute-done), channel_id=1, source_target_pairs={{4,0},{6,2},{8,4},{10,6},{12,8},{14,10},{0,12},{2,14},{5,1},{7,3},... | collective-permute-start | bytes 983048 | tf_op jit(solution)/shard_map/ppermute | solution.py:87
  42.2 15.3 %collective-permute-start.11 = (bf16[48,2048]{1,0:T(8,128)(2,1)S(1)}, bf16[48,2048]{1,0:T(8,128)(2,1)S(1)}, u32[]{:S(2)}, u32[]{:S(2)}) collective-permute-start(bf16[48,2048]{1,0:T(8,128)(2,1)S(1)} %collective-permute-done.10), channel_id=1, source_target_pairs={{4,0},{6,2},{8,4},{10,6},{12,8},{14,10},{0,12},{2,14},{5,1},{7,3},... | collective-permute-start | bytes 589832 | tf_op jit(solution)/shard_map/ppermute | solution.py:87
  57.5 21.5 %collective-permute-start.3 = (bf16[128,2048]{1,0:T(8,128)(2,1)S(1)}, bf16[128,2048]{1,0:T(8,128)(2,1)S(1)}, u32[]{:S(2)}, u32[]{:S(2)}) collective-permute-start(bf16[128,2048]{1,0:T(8,128)(2,1)S(1)} %collective-permute-done.2), channel_id=1, source_target_pairs={{4,0},{6,2},{8,4},{10,6},{12,8},{14,10},{0,12},{2,14},{5,1},{7,3},... | collective-permute-start | bytes 1572872 | tf_op jit(solution)/shard_map/ppermute | solution.py:87
  59.7 39.4 %collective-permute-start.17 = (f32[48,384]{1,0:T(8,128)S(1)}, f32[48,384]{1,0:T(8,128)S(1)}, u32[]{:S(2)}, u32[]{:S(2)}) collective-permute-start(f32[48,384]{1,0:T(8,128)S(1)} %get-tuple-element.25), channel_id=1, source_target_pairs={{0,1},{1,0},{2,3},{3,2},{4,5},{5,4},{6,7},{7,6},{8,9},{9,8},{10,11... | collective-permute-start | bytes 221192 | tf_op jit(solution)/shard_map/ppermute | solution.py:90
  60.6 17.7 %collective-permute-start.7 = (bf16[80,2048]{1,0:T(8,128)(2,1)S(1)}, bf16[80,2048]{1,0:T(8,128)(2,1)S(1)}, u32[]{:S(2)}, u32[]{:S(2)}) collective-permute-start(bf16[80,2048]{1,0:T(8,128)(2,1)S(1)} %collective-permute-done.6), channel_id=1, source_target_pairs={{4,0},{6,2},{8,4},{10,6},{12,8},{14,10},{0,12},{2,14},{5,1},{7,3},... | collective-permute-start | bytes 983048 | tf_op jit(solution)/shard_map/ppermute | solution.py:87
  62.0 37.2 %collective-permute-start.24 = (f32[128,384]{1,0:T(8,128)S(1)}, f32[128,384]{1,0:T(8,128)S(1)}, u32[]{:S(2)}, u32[]{:S(2)}) collective-permute-start(f32[128,384]{1,0:T(8,128)S(1)} %get-tuple-element.17), channel_id=1, source_target_pairs={{0,1},{1,0},{2,3},{3,2},{4,5},{5,4},{6,7},{7,6},{8,9},{9,8},{10,11... | collective-permute-start | bytes 589832 | tf_op jit(solution)/shard_map/ppermute | solution.py:90
  78.4 21.3 %collective-permute-start.21 = (f32[128,384]{1,0:T(8,128)S(1)}, f32[128,384]{1,0:T(8,128)S(1)}, u32[]{:S(2)}, u32[]{:S(2)}) collective-permute-start(f32[128,384]{1,0:T(8,128)S(1)} %get-tuple-element.18), channel_id=1, source_target_pairs={{0,1},{1,0},{2,3},{3,2},{4,5},{5,4},{6,7},{7,6},{8,9},{9,8},{10,11... | collective-permute-start | bytes 589832 | tf_op jit(solution)/shard_map/ppermute | solution.py:90
  92.2 9.0 %collective-permute-start.12 = (f32[48,384]{1,0:T(8,128)S(1)}, f32[48,384]{1,0:T(8,128)S(1)}, u32[]{:S(2)}, u32[]{:S(2)}) collective-permute-start(f32[48,384]{1,0:T(8,128)S(1)} %slice_select_fusion.14), channel_id=1, source_target_pairs={{0,1},{1,0},{2,3},{3,2},{4,5},{5,4},{6,7},{7,6},{8,9},{9,8},{10,11... | collective-permute-start | bytes 221192 | tf_op jit(solution)/shard_map/ppermute | solution.py:90
  92.8 1.4 %collective-permute-start.8 = (f32[80,384]{1,0:T(8,128)S(1)}, f32[80,384]{1,0:T(8,128)S(1)}, u32[]{:S(2)}, u32[]{:S(2)}) collective-permute-start(f32[80,384]{1,0:T(8,128)S(1)} %slice_select_fusion.11), channel_id=1, source_target_pairs={{0,1},{1,0},{2,3},{3,2},{4,5},{5,4},{6,7},{7,6},{8,9},{9,8},{10,11... | collective-permute-start | bytes 368648 | tf_op jit(solution)/shard_map/ppermute | solution.py:90
  94.2 1.4 %collective-permute-start.25 = (f32[128,384]{1,0:T(8,128)S(1)}, f32[128,384]{1,0:T(8,128)S(1)}, u32[]{:S(2)}, u32[]{:S(2)}) collective-permute-start(f32[128,384]{1,0:T(8,128)S(1)} %slice_select_fusion), channel_id=1, source_target_pairs={{0,1},{1,0},{2,3},{3,2},{4,5},{5,4},{6,7},{7,6},{8,9},{9,8},{10,11... | collective-permute-start | bytes 589832 | tf_op jit(solution)/shard_map/ppermute | solution.py:90
  95.6 1.4 %collective-permute-start.15 = (f32[128,384]{1,0:T(8,128)S(1)}, f32[128,384]{1,0:T(8,128)S(1)}, u32[]{:S(2)}, u32[]{:S(2)}) collective-permute-start(f32[128,384]{1,0:T(8,128)S(1)} %slice_select_fusion.6), channel_id=1, source_target_pairs={{0,1},{1,0},{2,3},{3,2},{4,5},{5,4},{6,7},{7,6},{8,9},{9,8},{10,11... | collective-permute-start | bytes 589832 | tf_op jit(solution)/shard_map/ppermute | solution.py:90
  97.1 1.4 %collective-permute-start.22 = (f32[128,384]{1,0:T(8,128)S(1)}, f32[128,384]{1,0:T(8,128)S(1)}, u32[]{:S(2)}, u32[]{:S(2)}) collective-permute-start(f32[128,384]{1,0:T(8,128)S(1)} %get-tuple-element.16), channel_id=1, source_target_pairs={{0,1},{1,0},{2,3},{3,2},{4,5},{5,4},{6,7},{7,6},{8,9},{9,8},{10,11... | collective-permute-start | bytes 589832 | tf_op jit(solution)/shard_map/ppermute | solution.py:90
  98.5 7.8 %collective-permute-start.26 = (f32[128,384]{1,0:T(8,128)S(1)}, f32[128,384]{1,0:T(8,128)S(1)}, u32[]{:S(2)}, u32[]{:S(2)}) collective-permute-start(f32[128,384]{1,0:T(8,128)S(1)} %get-tuple-element.15), channel_id=1, source_target_pairs={{0,2},{2,0},{4,6},{6,4},{8,10},{10,8},{12,14},{14,12},{1,3},{3,1},... | collective-permute-start | bytes 589832 | tf_op jit(solution)/shard_map/ppermute | solution.py:87
  99.1 18.8 %collective-permute-start.14 = (f32[80,384]{1,0:T(8,128)S(1)}, f32[80,384]{1,0:T(8,128)S(1)}, u32[]{:S(2)}, u32[]{:S(2)}) collective-permute-start(f32[80,384]{1,0:T(8,128)S(1)} %get-tuple-element.23), channel_id=1, source_target_pairs={{0,1},{1,0},{2,3},{3,2},{4,5},{5,4},{6,7},{7,6},{8,9},{9,8},{10,11... | collective-permute-start | bytes 368648 | tf_op jit(solution)/shard_map/ppermute | solution.py:90
  99.2 18.8 %collective-permute-start.4 = (f32[128,384]{1,0:T(8,128)S(1)}, f32[128,384]{1,0:T(8,128)S(1)}, u32[]{:S(2)}, u32[]{:S(2)}) collective-permute-start(f32[128,384]{1,0:T(8,128)S(1)} %get-tuple-element.21), channel_id=1, source_target_pairs={{0,1},{1,0},{2,3},{3,2},{4,5},{5,4},{6,7},{7,6},{8,9},{9,8},{10,11... | collective-permute-start | bytes 589832 | tf_op jit(solution)/shard_map/ppermute | solution.py:90
  99.7 21.2 %collective-permute-start.9 = (f32[80,384]{1,0:T(8,128)S(1)}, f32[80,384]{1,0:T(8,128)S(1)}, u32[]{:S(2)}, u32[]{:S(2)}) collective-permute-start(f32[80,384]{1,0:T(8,128)S(1)} %select_add_fusion.3), channel_id=1, source_target_pairs={{0,2},{2,0},{4,6},{6,4},{8,10},{10,8},{12,14},{14,12},{1,3},{3,1},... | collective-permute-start | bytes 368648 | tf_op jit(solution)/shard_map/ppermute | solution.py:87
  101.2 19.7 %collective-permute-start.16 = (f32[128,384]{1,0:T(8,128)S(1)}, f32[128,384]{1,0:T(8,128)S(1)}, u32[]{:S(2)}, u32[]{:S(2)}) collective-permute-start(f32[128,384]{1,0:T(8,128)S(1)} %select_add_fusion.2), channel_id=1, source_target_pairs={{0,2},{2,0},{4,6},{6,4},{8,10},{10,8},{12,14},{14,12},{1,3},{3,1},... | collective-permute-start | bytes 589832 | tf_op jit(solution)/shard_map/ppermute | solution.py:87
  106.3 10.2 %collective-permute-start.23 = (f32[128,384]{1,0:T(8,128)S(1)}, f32[128,384]{1,0:T(8,128)S(1)}, u32[]{:S(2)}, u32[]{:S(2)}) collective-permute-start(f32[128,384]{1,0:T(8,128)S(1)} %select_add_fusion.1), channel_id=1, source_target_pairs={{0,2},{2,0},{4,6},{6,4},{8,10},{10,8},{12,14},{14,12},{1,3},{3,1},... | collective-permute-start | bytes 589832 | tf_op jit(solution)/shard_map/ppermute | solution.py:87
  116.5 4.4 %collective-permute-start.13 = (f32[48,384]{1,0:T(8,128)S(1)}, f32[48,384]{1,0:T(8,128)S(1)}, u32[]{:S(2)}, u32[]{:S(2)}) collective-permute-start(f32[48,384]{1,0:T(8,128)S(1)} %select_add_fusion.4), channel_id=1, source_target_pairs={{0,2},{2,0},{4,6},{6,4},{8,10},{10,8},{12,14},{14,12},{1,3},{3,1},... | collective-permute-start | bytes 221192 | tf_op jit(solution)/shard_map/ppermute | solution.py:87
